TPU v7x, 32 devices: a whole 2x2x4 slice. The times are simulated.
32 devices in a mesh: chaos: 4 (over z), gx: 4 (over y, x), gy: 2 (over core).
Axes of the slice: x: 2, y: 2, z: 4, core: 2. Of those that a mesh axis runs over, the one named last changes fastest.
Arguments:
- lam_start: float32 [286, 16, 512], P(None, ('chaos', 'gy'), 'gx'), may hold values from -6 to 6
- adj_source: float32 [286, 16, 512], P(None, ('chaos', 'gy'), 'gx'), may hold values from -6 to 6
- coef_points: float32 [512, 4, 4, 512], P('chaos', None, 'gy', 'gx'), may hold values from 0.1 to 1
- quad_index: int32 [512, 10], replicated, may hold values from 0 to 3
- mode_index: int32 [286, 10], replicated, may hold values from 0 to 3, as said below
Outputs:
- lam_end: float32 [286, 16, 512], P(None, ('chaos', 'gy'), 'gx')
Inputs may be any that keep to these rules, and one draw needn't show every extreme that they name: `mode_index`: each row is a multi-index whose degrees sum to at most 3; each such multi-index of 10 inputs appears exactly once.
All inputs are finite; a program needn't handle non-finite values.
Results may differ from a plain program's by a relative error of at most 0.00011.
Values sent between devices are 32-bit elements; how exact they have to be, the bound alone decides.
A program may use at most 64 MiB of HBM per device.

v0:
```python
import math

import jax
import jax.numpy as jnp
from jax import lax
from jax.sharding import PartitionSpec as P

STEPS = 2


gauss_nodes = (-2.3344142183389773, -0.7419637843027259, 0.7419637843027259, 2.3344142183389773)
gauss_weights = (0.04587585476806849, 0.4541241452319315, 0.4541241452319315, 0.04587585476806849)
mass_shift = 1.0
relax_rate = 0.2
top_prec = lax.Precision.HIGHEST


def extended(shard, sides, width):
    for axis, dim in sides:
        size, length = (lax.axis_size(axis), shard.shape[dim])
        up = [(i, (i + 1) % size) for i in range(size)]
        down = [(j, i) for i, j in up]
        last = lax.slice_in_dim(shard, length - width, length, axis=dim)
        initial = lax.slice_in_dim(shard, 0, width, axis=dim)
        before = lax.ppermute(last, axis, up)
        after = lax.ppermute(initial, axis, down)
        shard = jnp.concatenate([before, shard, after], axis=dim)
    return shard


def tables(quad_index, mode_index):
    node_vals = jnp.array(gauss_nodes, jnp.float32)
    node_wts = jnp.array(gauss_weights, jnp.float32)
    hermite = jnp.stack(
        [
            jnp.ones_like(node_vals),
            node_vals,
            (node_vals * node_vals - 1.0) / math.sqrt(2.0),
            (node_vals * node_vals * node_vals - 3.0 * node_vals) / math.sqrt(6.0),
        ],
        0,
    )
    levels = jnp.arange(4, dtype=jnp.int32)
    quad_hot = (quad_index[:, :, None] == levels[None, None, :]).astype(jnp.float32)
    mode_hot = (mode_index[:, :, None] == levels[None, None, :]).astype(jnp.float32)
    at_nodes = jnp.einsum("qdk,nk->qdn", quad_hot, hermite, precision=top_prec)
    factors = jnp.einsum("qdn,pdn->qpd", at_nodes, mode_hot, precision=top_prec)
    chaos_basis = jnp.prod(factors, axis=2)
    point_wts = jnp.prod(jnp.sum(quad_hot * node_wts[None, None, :], axis=2), axis=1)
    point_wts = point_wts / jnp.sum(point_wts)
    back_map = chaos_basis * point_wts[:, None]
    return (chaos_basis, back_map)


def local(lam_start, adj_source, coef_points, quad_index, mode_index):
    chaos_basis, back_map = tables(quad_index, mode_index)
    modes = lam_start.shape[0]
    row_len = lam_start.shape[1]
    col_len = lam_start.shape[2]
    points = quad_index.shape[0]
    row_dev = lax.axis_index(("chaos", "gy"))
    row_devs = lax.axis_size(("chaos", "gy"))
    row_ids = lax.broadcasted_iota(jnp.int32, (row_len + 2, 1), 0)
    low_wall = (row_ids == 0) & (row_dev == 0)
    high_wall = (row_ids == row_len + 1) & (row_dev == row_devs - 1)
    keep_mask = jnp.where(low_wall | high_wall, 0.0, 1.0).astype(jnp.float32)
    lam_now = lam_start
    for repeat in range(STEPS):
        padded = extended(lam_now, ((("chaos", "gy"), 1), ("gx", 2)), 1) * keep_mask
        grad_x = (padded[:, 1:-1, 2:] - padded[:, 1:-1, :-2]) * 0.5
        grad_y = (padded[:, 2:, 1:-1] - padded[:, :-2, 1:-1]) * 0.5
        gradients = jnp.stack([grad_x, grad_y], 1)
        at_points = jnp.dot(
            chaos_basis,
            gradients.reshape(modes, -1),
            precision=top_prec,
            preferred_element_type=jnp.float32,
        )
        product = (
            lax.all_to_all(
                at_points.reshape(points, 2, 1, row_len, col_len),
                "chaos",
                split_axis=0,
                concat_axis=2,
                tiled=True,
            )
            * coef_points[:, None]
        )
        flux_points = lax.all_to_all(product, "chaos", split_axis=2, concat_axis=0, tiled=True)
        fluxes = jnp.dot(
            back_map.T,
            flux_points.reshape(points, -1),
            precision=top_prec,
            preferred_element_type=jnp.float32,
        ).reshape(modes, 2, row_len, col_len)
        flux_pad = extended(fluxes, ((("chaos", "gy"), 2), ("gx", 3)), 1) * keep_mask
        divergence = (flux_pad[:, 0, 1:-1, 2:] - flux_pad[:, 0, 1:-1, :-2]) * 0.5 + (
            flux_pad[:, 1, 2:, 1:-1] - flux_pad[:, 1, :-2, 1:-1]
        ) * 0.5
        lam_now = lam_now + relax_rate * (adj_source - (mass_shift * lam_now - divergence))
    return lam_now


def solution(mesh):
    placed = (
        P(None, ("chaos", "gy"), "gx"),
        P(None, ("chaos", "gy"), "gx"),
        P("chaos", None, "gy", "gx"),
        P(),
        P(),
    )
    return jax.shard_map(
        local, mesh=mesh, in_specs=placed, out_specs=P(None, ("chaos", "gy"), "gx"), check_vma=False
    )
```

profile of v0, /device:TPU:0, one launch (start us, length us, event | category | flops | bytes accessed | tf_op | source)
XLA Modules:
  0.0 213.9 jit_solution(210476485019297218)
XLA Ops:
  0.0 1.3 fusion.44
  1.9 4.1 %collective-permute-start.1 = (f32[286,1,128]{2,0,1:T(8,128)S(1)}, f32[286,1,128]{2,0,1:T(8,128)S(1)}, u32[]{:S(2)}, u32[]{:S(2)}) collective-permute-start(f32[286,1,128]{2,0,1:T(8,128)S(1)} %copy.113), channel_id=1, source_target_pairs={{1,0},{8,1},{9,8},{16,9},{17,16},{24,17},{25,24},{0,25},{3,2},{10,... | collective-permute-start | bytes 439304 | tf_op jit(solution)/shard_map/ppermute | solution.py:26
  6.2 2.6 %convolution_reduce_fusion = f32[286,512]{1,0:T(8,128)S(1)} fusion(f32[512,10,4]{0,2,1:T(4,128)S(1)} %fusion.34, s32[286,10]{0,1:T(8,128)S(1)} %copy-done.13), kind=kOutput, calls=%fused_computation.2 | convolution fusion | flops 71616688 | bytes 679088 | tf_op jit(solution)/shard_map/qdn,pdn->qpd/dot_general | solution.py:47
  9.7 3.0 %collective-permute-start.3 = (f32[286,4,1]{0,1,2:T(4,128)S(1)}, f32[286,4,1]{0,1,2:T(4,128)S(1)}, u32[]{:S(2)}, u32[]{:S(2)}) collective-permute-start(f32[286,4,1]{0,1,2:T(4,128)S(1)} %copy.73), channel_id=1, source_target_pairs={{2,0},{4,2},{6,4},{0,6},{3,1},{5,3},{7,5},{1,7},{10,8},{12,10},{14... | collective-permute-start | bytes 13736 | tf_op jit(solution)/shard_map/ppermute | solution.py:26
  12.7 4.5 %collective-permute-done.2 = f32[286,4,1]{0,1,2:T(4,128)S(1)} collective-permute-done((f32[286,4,1]{0,1,2:T(4,128)S(1)}, f32[286,4,1]{0,1,2:T(4,128)S(1)}, u32[]{:S(2)}, u32[]{:S(2)}) %collective-permute-start.2) | collective-permute-done | bytes 4608 | tf_op jit(solution)/shard_map/ppermute | solution.py:25
  17.7 0.5 maximum_multiply_fusion.2
  19.9 1.9 convolution_bitcast_fusion.1
  21.9 0.8 copy.78
  22.7 29.5 %all_to_all.66 = f32[512,2,1,2,128]{4,3,1,2,0:T(2,128)S(1)} all-to-all(f32[512,2,1,2,128]{4,3,1,2,0:T(2,128)S(1)} %copy.78), channel_id=1, replica_groups=mesh['chaos'=4,'gx'=4,'gy'=2] {'chaos'}, dimensions={0} | all-to-all | bytes 2097152 | tf_op jit(solution)/shard_map/all_to_all | solution.py:80
  52.1 1.7 broadcast_multiply_fusion.1
  53.9 3.8 %all-to-all-start.1 = ((f32[128,2,4,2,128]{4,3,1,0,2:T(2,128)}), f32[128,2,4,2,128]{4,3,1,0,2:T(2,128)S(1)}, u32[]{:S(2)}, u32[]{:S(2)}) async-start(f32[128,2,4,2,128]{4,3,1,0,2:T(2,128)} %broadcast_multiply_fusion.1), calls=%async_computation.1 | async-start | bytes 2097152 | tf_op jit(solution)/shard_map/all_to_all | solution.py:89
  57.9 0.6 reduce_sum.19
  58.5 0.6 broadcast_divide_fusion
  59.1 23.9 %all-to-all-done.1 = f32[128,2,4,2,128]{4,3,1,0,2:T(2,128)S(1)} async-done(((f32[128,2,4,2,128]{4,3,1,0,2:T(2,128)}), f32[128,2,4,2,128]{4,3,1,0,2:T(2,128)S(1)}, u32[]{:S(2)}, u32[]{:S(2)}) %all-to-all-start.1) | async-done | bytes 1048608 | tf_op jit(solution)/shard_map/all_to_all | solution.py:89
  83.0 0.8 reshape.79
  84.2 1.2 fusion.4
  85.5 3.5 %collective-permute-start.5 = (f32[286,2,1,128]{3,0,2,1:T(8,128)S(1)}, f32[286,2,1,128]{3,0,2,1:T(8,128)S(1)}, u32[]{:S(2)}, u32[]{:S(2)}) collective-permute-start(f32[286,2,1,128]{3,0,2,1:T(8,128)S(1)} %get-tuple-element.18), channel_id=1, source_target_pairs={{1,0},{8,1},{9,8},{16,9},{17,16},{24,17},{25,24},{0,25},{3,2},{10,... | collective-permute-start | bytes 878600 | tf_op jit(solution)/shard_map/ppermute | solution.py:26
  89.0 7.5 %collective-permute-done.4 = f32[286,2,1,128]{3,0,2,1:T(8,128)S(1)} collective-permute-done((f32[286,2,1,128]{3,0,2,1:T(8,128)S(1)}, f32[286,2,1,128]{3,0,2,1:T(8,128)S(1)}, u32[]{:S(2)}, u32[]{:S(2)}) %collective-permute-start.4) | collective-permute-done | bytes 292896 | tf_op jit(solution)/shard_map/ppermute | solution.py:25
  96.5 0.7 copy-done.4
  97.2 0.7 copy-done.5
  99.4 2.9 %collective-permute-start.7 = (f32[286,2,4,1]{0,2,3,1:T(4,128)S(1)}, f32[286,2,4,1]{0,2,3,1:T(4,128)}, u32[]{:S(2)}, u32[]{:S(2)}) collective-permute-start(f32[286,2,4,1]{0,2,3,1:T(4,128)S(1)} %copy.82), channel_id=1, source_target_pairs={{2,0},{4,2},{6,4},{0,6},{3,1},{5,3},{7,5},{1,7},{10,8},{12,10},{14... | collective-permute-start | bytes 27464 | tf_op jit(solution)/shard_map/ppermute | solution.py:26
  102.3 1.2 collective-permute-done.6
  103.9 1.1 copy.84
  105.0 2.1 maximum_multiply_fusion
  107.6 3.5 %collective-permute-start.9 = (f32[286,1,128]{2,0,1:T(8,128)S(1)}, f32[286,1,128]{2,0,1:T(8,128)S(1)}, u32[]{:S(2)}, u32[]{:S(2)}) collective-permute-start(f32[286,1,128]{2,0,1:T(8,128)S(1)} %get-tuple-element.22), channel_id=1, source_target_pairs={{1,0},{8,1},{9,8},{16,9},{17,16},{24,17},{25,24},{0,25},{3,2},{10,... | collective-permute-start | bytes 439304 | tf_op jit(solution)/shard_map/ppermute | solution.py:26
  111.1 2.8 %collective-permute-done.8 = f32[286,1,128]{2,0,1:T(8,128)S(1)} collective-permute-done((f32[286,1,128]{2,0,1:T(8,128)S(1)}, f32[286,1,128]{2,0,1:T(8,128)S(1)}, u32[]{:S(2)}, u32[]{:S(2)}) %collective-permute-start.8) | collective-permute-done | bytes 146464 | tf_op jit(solution)/shard_map/ppermute | solution.py:25
  114.4 2.2 %collective-permute-start.10 = (f32[286,4,1]{0,1,2:T(4,128)S(1)}, f32[286,4,1]{0,1,2:T(4,128)S(1)}, u32[]{:S(2)}, u32[]{:S(2)}) collective-permute-start(f32[286,4,1]{0,1,2:T(4,128)S(1)} %copy.88), channel_id=1, source_target_pairs={{0,2},{2,4},{4,6},{6,0},{1,3},{3,5},{5,7},{7,1},{8,10},{10,12},{12... | collective-permute-start | bytes 13736 | tf_op jit(solution)/shard_map/ppermute | solution.py:25
  116.9 1.0 collective-permute-start.11
  117.9 1.3 collective-permute-done.10
  119.4 1.1 collective-permute-done.11
  123.0 1.9 convolution_bitcast_fusion
  124.9 0.8 copy.94
  125.7 29.6 %all_to_all.67 = f32[512,2,1,2,128]{4,3,1,2,0:T(2,128)S(1)} all-to-all(f32[512,2,1,2,128]{4,3,1,2,0:T(2,128)S(1)} %copy.94), channel_id=1, replica_groups=mesh['chaos'=4,'gx'=4,'gy'=2] {'chaos'}, dimensions={0} | all-to-all | bytes 2097152 | tf_op jit(solution)/shard_map/all_to_all | solution.py:80
  155.4 0.8 broadcast_multiply_fusion
  156.1 28.6 %all_to_all.68 = f32[128,2,4,2,128]{4,3,1,0,2:T(2,128)S(1)} all-to-all(f32[128,2,4,2,128]{4,3,1,0,2:T(2,128)S(1)} %broadcast_multiply_fusion), channel_id=1, replica_groups=mesh['chaos'=4,'gx'=4,'gy'=2] {'chaos'}, dimensions={2} | all-to-all | bytes 2097152 | tf_op jit(solution)/shard_map/all_to_all | solution.py:89
  184.7 1.8 reshape.82
  186.6 1.6 copy.95
  188.1 1.2 fusion.2
  189.4 3.5 %collective-permute-start.13 = (f32[286,2,1,128]{3,0,2,1:T(8,128)S(1)}, f32[286,2,1,128]{3,0,2,1:T(8,128)S(1)}, u32[]{:S(2)}, u32[]{:S(2)}) collective-permute-start(f32[286,2,1,128]{3,0,2,1:T(8,128)S(1)} %get-tuple-element.14), channel_id=1, source_target_pairs={{1,0},{8,1},{9,8},{16,9},{17,16},{24,17},{25,24},{0,25},{3,2},{10,... | collective-permute-start | bytes 878600 | tf_op jit(solution)/shard_map/ppermute | solution.py:26
  192.9 7.5 %collective-permute-done.12 = f32[286,2,1,128]{3,0,2,1:T(8,128)S(1)} collective-permute-done((f32[286,2,1,128]{3,0,2,1:T(8,128)S(1)}, f32[286,2,1,128]{3,0,2,1:T(8,128)S(1)}, u32[]{:S(2)}, u32[]{:S(2)}) %collective-permute-start.12) | collective-permute-done | bytes 292896 | tf_op jit(solution)/shard_map/ppermute | solution.py:25
  200.5 1.4 fusion.37
  202.0 1.7 copy.96
  203.7 1.0 collective-permute-start.14
  205.2 2.0 collective-permute-start.15
  207.1 1.2 collective-permute-done.14
  208.9 1.4 copy.99
  210.3 2.3 %maximum_multiply_fusion.1 = f32[286,2,4,130]{3,0,2,1:T(8,128)S(1)} fusion(f32[286,2,4,1]{3,0,2,1:T(8,128)} %copy.99, f32[286,2,1,128]{3,0,2,1:T(8,128)S(1)} %collective-permute-done.13, f32[286,2,2,128]{3,0,2,1:T(8,128)S(1)} %fusion.2, f32[286,2,1,128]{3,0,2,1:T(8,128)S(1)} %collective-permute-done.12, f32[286,2,4,1]{3,0,2,1:T(8,128)S(1)} %copy.98, ...), kind=kLoop, calls=%fused_computation.1 | loop fusion | flops 1487200 | bytes 2379536 | tf_op jit(solution)/shard_map/mul | solution.py:96
  212.9 0.9 copy.101
  (85 shorter events, 11.4 us)
Async XLA Ops:
  0.0 6.0 %copy-start.11 = (f32[4,4,1]{1,0,2:T(4,128)S(1)}, f32[4,4,1]{1,0,2:T(4,128)}, u32[]{:S(2)}) copy-start(f32[4,4,1]{1,0,2:T(4,128)} %constant.58) | copy-start | bytes 196
  0.0 6.0 %copy-start.8 = (s32[512,10]{0,1:T(8,128)S(1)}, s32[512,10]{0,1:T(8,128)}, u32[]{:S(2)}) copy-start(s32[512,10]{0,1:T(8,128)} %param.10) | copy-start | bytes 61444
  0.0 6.2 %copy-start.13 = (s32[286,10]{0,1:T(8,128)S(1)}, s32[286,10]{0,1:T(8,128)}, u32[]{:S(2)}) copy-start(s32[286,10]{0,1:T(8,128)} %param.11) | copy-start | bytes 34324
  1.3 7.6 %copy-start = (f32[286,2,128]{2,1,0:T(2,128)S(1)}, f32[286,2,128]{2,1,0:T(2,128)}, u32[]{:S(2)}) copy-start(f32[286,2,128]{2,1,0:T(2,128)} %param.7) | copy-start | bytes 878596
  1.4 7.5 %collective-permute-start = (f32[286,1,128]{2,0,1:T(8,128)S(1)}, f32[286,1,128]{2,0,1:T(8,128)S(1)}, u32[]{:S(2)}, u32[]{:S(2)}) collective-permute-start(f32[286,1,128]{2,0,1:T(8,128)S(1)} %copy.112), channel_id=1, source_target_pairs={{0,1},{1,8},{8,9},{9,16},{16,17},{17,24},{24,25},{25,0},{2,3},{3,1... | collective-permute-start | bytes 439304 | tf_op jit(solution)/shard_map/ppermute | solution.py:25
  1.9 7.0 %collective-permute-start.1 = (f32[286,1,128]{2,0,1:T(8,128)S(1)}, f32[286,1,128]{2,0,1:T(8,128)S(1)}, u32[]{:S(2)}, u32[]{:S(2)}) collective-permute-start(f32[286,1,128]{2,0,1:T(8,128)S(1)} %copy.113), channel_id=1, source_target_pairs={{1,0},{8,1},{9,8},{16,9},{17,16},{24,17},{25,24},{0,25},{3,2},{10,... | collective-permute-start | bytes 439304 | tf_op jit(solution)/shard_map/ppermute | solution.py:26
  9.7 7.8 %collective-permute-start.3 = (f32[286,4,1]{0,1,2:T(4,128)S(1)}, f32[286,4,1]{0,1,2:T(4,128)S(1)}, u32[]{:S(2)}, u32[]{:S(2)}) collective-permute-start(f32[286,4,1]{0,1,2:T(4,128)S(1)} %copy.73), channel_id=1, source_target_pairs={{2,0},{4,2},{6,4},{0,6},{3,1},{5,3},{7,5},{1,7},{10,8},{12,10},{14... | collective-permute-start | bytes 13736 | tf_op jit(solution)/shard_map/ppermute | solution.py:26
  12.7 4.6 %collective-permute-start.2 = (f32[286,4,1]{0,1,2:T(4,128)S(1)}, f32[286,4,1]{0,1,2:T(4,128)S(1)}, u32[]{:S(2)}, u32[]{:S(2)}) collective-permute-start(f32[286,4,1]{0,1,2:T(4,128)S(1)} %copy.72), channel_id=1, source_target_pairs={{0,2},{2,4},{4,6},{6,0},{1,3},{3,5},{5,7},{7,1},{8,10},{10,12},{12... | collective-permute-start | bytes 13736 | tf_op jit(solution)/shard_map/ppermute | solution.py:25
  12.7 5.6 %copy-start.9 = (f32[4]{0:T(128)}, f32[4]{0:T(128)S(1)}, u32[]{:S(2)}) copy-start(f32[4]{0:T(128)S(1)} %or_select_fusion) | copy-start | bytes 52
  22.7 29.5 %copy-start.2 = (f32[128,4,2,128]{3,2,1,0:T(2,128)S(1)}, f32[128,4,2,128]{3,2,1,0:T(2,128)}, u32[]{:S(2)}) copy-start(f32[128,4,2,128]{3,2,1,0:T(2,128)} %param.9) | copy-start | bytes 1572868
  53.9 3.8 %copy-start.12 = (f32[4]{0:T(128)S(1)}, f32[4]{0:T(128)}, u32[]{:S(2)}) copy-start(f32[4]{0:T(128)} %constant.44.clone) | copy-start | bytes 52
  53.9 29.1 %all-to-all-start.1 = ((f32[128,2,4,2,128]{4,3,1,0,2:T(2,128)}), f32[128,2,4,2,128]{4,3,1,0,2:T(2,128)S(1)}, u32[]{:S(2)}, u32[]{:S(2)}) async-start(f32[128,2,4,2,128]{4,3,1,0,2:T(2,128)} %broadcast_multiply_fusion.1), calls=%async_computation.1 | async-start | bytes 2097152 | tf_op jit(solution)/shard_map/all_to_all | solution.py:89
  85.4 11.1 %collective-permute-start.4 = (f32[286,2,1,128]{3,0,2,1:T(8,128)S(1)}, f32[286,2,1,128]{3,0,2,1:T(8,128)S(1)}, u32[]{:S(2)}, u32[]{:S(2)}) collective-permute-start(f32[286,2,1,128]{3,0,2,1:T(8,128)S(1)} %get-tuple-element.17), channel_id=1, source_target_pairs={{0,1},{1,8},{8,9},{9,16},{16,17},{17,24},{24,25},{25,0},{2,3},{3,1... | collective-permute-start | bytes 878600 | tf_op jit(solution)/shard_map/ppermute | solution.py:25
  85.5 11.1 %collective-permute-start.5 = (f32[286,2,1,128]{3,0,2,1:T(8,128)S(1)}, f32[286,2,1,128]{3,0,2,1:T(8,128)S(1)}, u32[]{:S(2)}, u32[]{:S(2)}) collective-permute-start(f32[286,2,1,128]{3,0,2,1:T(8,128)S(1)} %get-tuple-element.18), channel_id=1, source_target_pairs={{1,0},{8,1},{9,8},{16,9},{17,16},{24,17},{25,24},{0,25},{3,2},{10,... | collective-permute-start | bytes 878600 | tf_op jit(solution)/shard_map/ppermute | solution.py:26
  96.5 0.7 copy-start.4
  97.2 0.7 copy-start.5
  98.9 4.6 %collective-permute-start.6 = (f32[286,2,4,1]{0,2,3,1:T(4,128)S(1)}, f32[286,2,4,1]{0,2,3,1:T(4,128)S(1)}, u32[]{:S(2)}, u32[]{:S(2)}) collective-permute-start(f32[286,2,4,1]{0,2,3,1:T(4,128)S(1)} %copy.81), channel_id=1, source_target_pairs={{0,2},{2,4},{4,6},{6,0},{1,3},{3,5},{5,7},{7,1},{8,10},{10,12},{12... | collective-permute-start | bytes 27464 | tf_op jit(solution)/shard_map/ppermute | solution.py:25
  99.4 4.5 %collective-permute-start.7 = (f32[286,2,4,1]{0,2,3,1:T(4,128)S(1)}, f32[286,2,4,1]{0,2,3,1:T(4,128)}, u32[]{:S(2)}, u32[]{:S(2)}) collective-permute-start(f32[286,2,4,1]{0,2,3,1:T(4,128)S(1)} %copy.82), channel_id=1, source_target_pairs={{2,0},{4,2},{6,4},{0,6},{3,1},{5,3},{7,5},{1,7},{10,8},{12,10},{14... | collective-permute-start | bytes 27464 | tf_op jit(solution)/shard_map/ppermute | solution.py:26
  105.0 2.1 copy-start.1
  105.0 2.1 copy-start.6
  107.5 6.4 %collective-permute-start.8 = (f32[286,1,128]{2,0,1:T(8,128)S(1)}, f32[286,1,128]{2,0,1:T(8,128)S(1)}, u32[]{:S(2)}, u32[]{:S(2)}) collective-permute-start(f32[286,1,128]{2,0,1:T(8,128)S(1)} %get-tuple-element.21), channel_id=1, source_target_pairs={{0,1},{1,8},{8,9},{9,16},{16,17},{17,24},{24,25},{25,0},{2,3},{3,1... | collective-permute-start | bytes 439304 | tf_op jit(solution)/shard_map/ppermute | solution.py:25
  107.6 6.4 %collective-permute-start.9 = (f32[286,1,128]{2,0,1:T(8,128)S(1)}, f32[286,1,128]{2,0,1:T(8,128)S(1)}, u32[]{:S(2)}, u32[]{:S(2)}) collective-permute-start(f32[286,1,128]{2,0,1:T(8,128)S(1)} %get-tuple-element.22), channel_id=1, source_target_pairs={{1,0},{8,1},{9,8},{16,9},{17,16},{24,17},{25,24},{0,25},{3,2},{10,... | collective-permute-start | bytes 439304 | tf_op jit(solution)/shard_map/ppermute | solution.py:26
  114.2 6.6 %copy-start.10 = (f32[4]{0:T(128)S(1)}, f32[4]{0:T(128)}, u32[]{:S(2)}) copy-start(f32[4]{0:T(128)} %copy-done.9) | copy-start | bytes 52
  114.4 4.7 %collective-permute-start.10 = (f32[286,4,1]{0,1,2:T(4,128)S(1)}, f32[286,4,1]{0,1,2:T(4,128)S(1)}, u32[]{:S(2)}, u32[]{:S(2)}) collective-permute-start(f32[286,4,1]{0,1,2:T(4,128)S(1)} %copy.88), channel_id=1, source_target_pairs={{0,2},{2,4},{4,6},{6,0},{1,3},{3,5},{5,7},{7,1},{8,10},{10,12},{12... | collective-permute-start | bytes 13736 | tf_op jit(solution)/shard_map/ppermute | solution.py:25
  116.9 3.6 %collective-permute-start.11 = (f32[286,4,1]{0,1,2:T(4,128)S(1)}, f32[286,4,1]{0,1,2:T(4,128)S(1)}, u32[]{:S(2)}, u32[]{:S(2)}) collective-permute-start(f32[286,4,1]{0,1,2:T(4,128)S(1)} %copy.89), channel_id=1, source_target_pairs={{2,0},{4,2},{6,4},{0,6},{3,1},{5,3},{7,5},{1,7},{10,8},{12,10},{14... | collective-permute-start | bytes 13736 | tf_op jit(solution)/shard_map/ppermute | solution.py:26
  125.7 29.7 %copy-start.3 = (f32[128,4,2,128]{3,2,1,0:T(2,128)S(1)}, f32[128,4,2,128]{3,2,1,0:T(2,128)}, u32[]{:S(2)}) copy-start(f32[128,4,2,128]{3,2,1,0:T(2,128)} %param.9) | copy-start | bytes 1572868
  189.3 11.1 %collective-permute-start.12 = (f32[286,2,1,128]{3,0,2,1:T(8,128)S(1)}, f32[286,2,1,128]{3,0,2,1:T(8,128)S(1)}, u32[]{:S(2)}, u32[]{:S(2)}) collective-permute-start(f32[286,2,1,128]{3,0,2,1:T(8,128)S(1)} %get-tuple-element.13), channel_id=1, source_target_pairs={{0,1},{1,8},{8,9},{9,16},{16,17},{17,24},{24,25},{25,0},{2,3},{3,1... | collective-permute-start | bytes 878600 | tf_op jit(solution)/shard_map/ppermute | solution.py:25
  189.4 11.1 %collective-permute-start.13 = (f32[286,2,1,128]{3,0,2,1:T(8,128)S(1)}, f32[286,2,1,128]{3,0,2,1:T(8,128)S(1)}, u32[]{:S(2)}, u32[]{:S(2)}) collective-permute-start(f32[286,2,1,128]{3,0,2,1:T(8,128)S(1)} %get-tuple-element.14), channel_id=1, source_target_pairs={{1,0},{8,1},{9,8},{16,9},{17,16},{24,17},{25,24},{0,25},{3,2},{10,... | collective-permute-start | bytes 878600 | tf_op jit(solution)/shard_map/ppermute | solution.py:26
  203.7 4.6 %collective-permute-start.14 = (f32[286,2,4,1]{0,2,3,1:T(4,128)S(1)}, f32[286,2,4,1]{0,2,3,1:T(4,128)S(1)}, u32[]{:S(2)}, u32[]{:S(2)}) collective-permute-start(f32[286,2,4,1]{0,2,3,1:T(4,128)S(1)} %copy.96), channel_id=1, source_target_pairs={{0,2},{2,4},{4,6},{6,0},{1,3},{3,5},{5,7},{7,1},{8,10},{10,12},{12... | collective-permute-start | bytes 27464 | tf_op jit(solution)/shard_map/ppermute | solution.py:25
  205.2 3.7 %collective-permute-start.15 = (f32[286,2,4,1]{0,2,3,1:T(4,128)S(1)}, f32[286,2,4,1]{0,2,3,1:T(4,128)S(1)}, u32[]{:S(2)}, u32[]{:S(2)}) collective-permute-start(f32[286,2,4,1]{0,2,3,1:T(4,128)S(1)} %copy.97), channel_id=1, source_target_pairs={{2,0},{4,2},{6,4},{0,6},{3,1},{5,3},{7,5},{1,7},{10,8},{12,10},{14... | collective-permute-start | bytes 27464 | tf_op jit(solution)/shard_map/ppermute | solution.py:26
  210.3 2.3 %copy-start.7 = (f32[286,2,128]{2,1,0:T(2,128)S(1)}, f32[286,2,128]{2,1,0:T(2,128)}, u32[]{:S(2)}) copy-start(f32[286,2,128]{2,1,0:T(2,128)} %param.8) | copy-start | bytes 878596
where the time goes:
time: 214 us
  blocking collectives  87.7 us (41%)
  waiting for transfers between devices  51.2 us (24%)
  starting transfers between devices  31.2 us (15%)
  local copies, waits for them, and re-layouts  23.4 us (11%)
  other arithmetic  10.8 us (5%)
  matrix products  8.97 us (4%)
    all_to_all x2, blocking collectives, local(): lax.all_to_all(at_points.reshape(points, 2, 1, row_len, col_len), 'chaos'...  59.1 us
    all_to_all x1, blocking collectives, local(): lax.all_to_all(product, 'chaos', split_axis=2, concat_axis=0, tiled=True)  28.6 us
    ppermute x8, waiting for transfers between devices, extended(): before = lax.ppermute(last, axis, up)  26.1 us
    all_to_all x1, waiting for transfers between devices, local(): lax.all_to_all(product, 'chaos', split_axis=2, concat_axis=0, tiled=True)  23.9 us
    ppermute x8, starting transfers between devices, extended(): after = lax.ppermute(initial, axis, down)  23.5 us
    slice x11, local copies, waits for them, and re-layouts, extended(): last = lax.slice_in_dim(shard, length - width, length, axis=dim)  5.06 us
    mul x2, other arithmetic, local(): extended(fluxes, ((('chaos', 'gy'), 2), ('gx', 3)), 1) * keep_mask  4.39 us
  transfers between devices with their start and end apart: 17, of which 10 were waited for; matrix products, arithmetic and copies ran while one was open for 3% of the time, Pallas kernels for 0%

commit v1 on v0

v1 whole, which is shorter than its diff:
```python
import math

import jax
import jax.numpy as jnp
from jax import lax
from jax.sharding import PartitionSpec as P

STEPS = 2


gauss_nodes = (-2.3344142183389773, -0.7419637843027259, 0.7419637843027259, 2.3344142183389773)
gauss_weights = (0.04587585476806849, 0.4541241452319315, 0.4541241452319315, 0.04587585476806849)
mass_shift = 1.0
relax_rate = 0.2
top_prec = lax.Precision.HIGHEST


def tables(quad_index, mode_index):
    node_vals = jnp.array(gauss_nodes, jnp.float32)
    node_wts = jnp.array(gauss_weights, jnp.float32)
    hermite = jnp.stack(
        [
            jnp.ones_like(node_vals),
            node_vals,
            (node_vals * node_vals - 1.0) / math.sqrt(2.0),
            (node_vals * node_vals * node_vals - 3.0 * node_vals) / math.sqrt(6.0),
        ],
        0,
    )
    levels = jnp.arange(4, dtype=jnp.int32)
    quad_hot = (quad_index[:, :, None] == levels[None, None, :]).astype(jnp.float32)
    mode_hot = (mode_index[:, :, None] == levels[None, None, :]).astype(jnp.float32)
    at_nodes = jnp.einsum("qdk,nk->qdn", quad_hot, hermite, precision=top_prec)
    factors = jnp.einsum("qdn,pdn->qpd", at_nodes, mode_hot, precision=top_prec)
    chaos_basis = jnp.prod(factors, axis=2)
    point_wts = jnp.prod(jnp.sum(quad_hot * node_wts[None, None, :], axis=2), axis=1)
    point_wts = point_wts / jnp.sum(point_wts)
    back_map = chaos_basis * point_wts[:, None]
    return (chaos_basis, back_map)


def shift_pair(low, high, axis):
    size = lax.axis_size(axis)
    up = [(i, (i + 1) % size) for i in range(size)]
    down = [(j, i) for i, j in up]
    return lax.ppermute(high, axis, up), lax.ppermute(low, axis, down)


def local(lam_start, adj_source, coef_points, quad_index, mode_index):
    modes, row_len, col_len = lam_start.shape
    points = quad_index.shape[0]
    rows = ("chaos", "gy")
    row_dev = lax.axis_index(rows)
    row_devs = lax.axis_size(rows)
    keep_low = jnp.where(row_dev == 0, 0.0, 1.0).astype(jnp.float32)
    keep_high = jnp.where(row_dev == row_devs - 1, 0.0, 1.0).astype(jnp.float32)
    coef = lax.all_to_all(coef_points, "chaos", split_axis=1, concat_axis=0, tiled=True)
    coef = coef.reshape(points, row_len, col_len)
    k_low, k_high = shift_pair(coef[:, 0], coef[:, -1], rows)
    k_left, k_right = shift_pair(coef[:, :, :1], coef[:, :, -1:], "gx")
    chaos_basis, back_map = tables(quad_index, mode_index)
    coef_y = [k_low * keep_low] + [coef[:, r] for r in range(row_len)] + [k_high * keep_high]
    coef_x = [jnp.concatenate([k_left[:, r], coef[:, r], k_right[:, r]], 1) for r in range(row_len)]
    lam_now = lam_start
    for repeat in range(STEPS):
        v_low, v_high = shift_pair(lam_now[:, :2], lam_now[:, -2:], rows)
        v_left, v_right = shift_pair(lam_now[:, :, :2], lam_now[:, :, -2:], "gx")
        v_low = v_low * keep_low
        v_high = v_high * keep_high
        parts = [v_low[:, 0], v_low[:, 1]] + [lam_now[:, r] for r in range(row_len)] + [v_high[:, 0], v_high[:, 1]]
        edges = [v_left[:, r] for r in range(row_len)] + [v_right[:, r] for r in range(row_len)]
        u = jnp.dot(chaos_basis, jnp.concatenate(parts + edges, 1), precision=top_prec, preferred_element_type=jnp.float32)
        u_row = [u[:, i * col_len : (i + 1) * col_len] for i in range(row_len + 4)]
        base = (row_len + 4) * col_len
        u_left = [u[:, base + 2 * r : base + 2 * r + 2] for r in range(row_len)]
        base += 2 * row_len
        u_right = [u[:, base + 2 * r : base + 2 * r + 2] for r in range(row_len)]
        flux_y = [coef_y[i] * ((u_row[i + 2] - u_row[i]) * 0.5) for i in range(row_len + 2)]
        div = []
        for r in range(row_len):
            wide = jnp.concatenate([u_left[r], u_row[r + 2], u_right[r]], 1)
            flux_x = coef_x[r] * ((wide[:, 2:] - wide[:, :-2]) * 0.5)
            div.append((flux_x[:, 2:] - flux_x[:, :-2]) * 0.5 + (flux_y[r + 2] - flux_y[r]) * 0.5)
        back = jnp.dot(back_map.T, jnp.concatenate(div, 1), precision=top_prec, preferred_element_type=jnp.float32)
        divergence = back.reshape(modes, row_len, col_len)
        lam_now = lam_now + relax_rate * (adj_source - (mass_shift * lam_now - divergence))
    return lam_now


def solution(mesh):
    placed = (
        P(None, ("chaos", "gy"), "gx"),
        P(None, ("chaos", "gy"), "gx"),
        P("chaos", None, "gy", "gx"),
        P(),
        P(),
    )
    return jax.shard_map(
        local, mesh=mesh, in_specs=placed, out_specs=P(None, ("chaos", "gy"), "gx"), check_vma=False
    )
```

time: 214 us -> 81.1 us (0.38)
  blocking collectives: 87.7 us -> 0 us
  waiting for transfers between devices: 51.2 us -> 25.1 us
  starting transfers between devices: 31.2 us -> 20 us
  local copies, waits for them, and re-layouts: 23.4 us -> 16.1 us
  other arithmetic: 10.8 us -> 7.13 us
  matrix products: 8.97 us -> 11.6 us
    all_to_all x3 -> x0, blocking collectives: 87.7 us -> none  [the longest x2 59.1 us: local(): lax.all_to_all(at_points.reshape(points, 2, 1, row_len, col_len), 'chaos'...]
    all_to_all x1, waiting for transfers between devices: 23.9 us -> 0.01 us  [local(): lax.all_to_all(coef_points, 'chaos', split_axis=1, concat_axis=0, tiled=T...]
    ppermute x16 -> x12, starting transfers between devices: 27.4 us -> 16.4 us  [shift_pair(): return (lax.ppermute(high, axis, up), lax.ppermute(low, axis, down))]
    mul x6 -> x8, other arithmetic: 7.94 us -> 0.41 us  [the longest x4 0.32 us: local(): flux_x = coef_x[r] * ((wide[:, 2:] - wide[:, :-2]) * 0.5)]
    unnamed x32 -> x40, local copies, waits for them, and re-layouts: 1.53 us -> 7.13 us
    slice x16 -> x9, local copies, waits for them, and re-layouts: 7.85 us -> 2.87 us  [the longest x1 1.36 us: local(): k_left, k_right = shift_pair(coef[:, :, :1], coef[:, :, -1:], 'gx')]
    add x0 -> x4, other arithmetic: none -> 4.61 us  [local(): (flux_x[:, 2:] - flux_x[:, :-2]) * 0.5 + (flux_y[r + 2] - flux_y[r]) * 0.5]
    ppermute x8 -> x0, local copies, waits for them, and re-layouts: 4.3 us -> none  [the longest x4 3.02 us: extended(): after = lax.ppermute(initial, axis, down)]
  transfers between devices with their start and end apart: 17 -> 13, of which waited for: 10 -> 5; matrix products, arithmetic and copies ran while one was open for 3% -> 24% of each run, Pallas kernels for 0% -> 0%
where the time goes in v1:
time: 81.1 us; the launch traced here: 80.5 us
  waiting for transfers between devices  25.1 us (31%)
  starting transfers between devices  20 us (25%)
  local copies, waits for them, and re-layouts  16.1 us (20%)
  matrix products  11.6 us (14%)
  other arithmetic  7.13 us (9%)
    ppermute x12, waiting for transfers between devices, shift_pair(): return (lax.ppermute(high, axis, up), lax.ppermute(low, axis, down))  25.1 us
    ppermute x12, starting transfers between devices, shift_pair(): return (lax.ppermute(high, axis, up), lax.ppermute(low, axis, down))  16.4 us
    unnamed x40, local copies, waits for them, and re-layouts  7.13 us
    dot_general x2, matrix products, local(): jnp.dot(chaos_basis, jnp.concatenate(parts + edges, 1), precision=top_pre...  6.67 us
    add x4, other arithmetic, local(): (flux_x[:, 2:] - flux_x[:, :-2]) * 0.5 + (flux_y[r + 2] - flux_y[r]) * 0.5  4.61 us
    all_to_all x1, starting transfers between devices, local(): lax.all_to_all(coef_points, 'chaos', split_axis=1, concat_axis=0, tiled=T...  3.6 us
    dot_general x1, matrix products, tables(): factors = jnp.einsum('qdn,pdn->qpd', at_nodes, mode_hot, precision=top_prec)  3.4 us
    concatenate x2, local copies, waits for them, and re-layouts, local(): jnp.concatenate(parts + edges, 1)  2.57 us
  transfers between devices with their start and end apart: 13, of which 5 were waited for; matrix products, arithmetic and copies ran while one was open for 24% of the time, Pallas kernels for 0%

profile of v1, /device:TPU:0, one launch (start us, length us, event | category | flops | bytes accessed | tf_op | source)
XLA Modules:
  0.0 80.5 jit_solution(6977557665041020564)
XLA Ops:
  0.0 1.0 %copy.78 = f32[286,2,128]{2,0,1:T(8,128)S(1)} copy(f32[286,2,128]{2,1,0:T(2,128)} %param.7) | data formatting | bytes 585728 | tf_op args[0]
  1.0 4.5 %collective-permute-start.3 = (f32[286,2,128]{2,0,1:T(8,128)S(1)}, f32[286,2,128]{2,0,1:T(8,128)S(1)}, u32[]{:S(2)}, u32[]{:S(2)}) collective-permute-start(f32[286,2,128]{2,0,1:T(8,128)S(1)} %copy.78), channel_id=1, source_target_pairs={{1,0},{8,1},{9,8},{16,9},{17,16},{24,17},{25,24},{0,25},{3,2},{10,... | collective-permute-start | bytes 878600 | tf_op jit(solution)/shard_map/ppermute | solution.py:46
  5.5 2.0 %copy.67 = f32[128,4,2,128]{3,2,0,1:T(2,128)} copy(f32[128,4,2,128]{3,2,1,0:T(2,128)} %param.9) | data formatting | bytes 1048576 | tf_op args[2]
  7.6 3.6 %all-to-all-start = ((f32[128,4,2,128]{3,2,0,1:T(2,128)}), f32[128,4,2,128]{3,2,0,1:T(2,128)S(1)}, u32[]{:S(2)}, u32[]{:S(2)}) async-start(f32[128,4,2,128]{3,2,0,1:T(2,128)} %copy.67), calls=%async_computation | async-start | bytes 1048576 | tf_op jit(solution)/shard_map/all_to_all | solution.py:57
  11.2 0.1 fusion.64
  11.3 2.5 %collective-permute-start.5 = (f32[286,2,2]{2,0,1:T(8,128)S(1)}, f32[286,2,2]{2,0,1:T(8,128)S(1)}, u32[]{:S(2)}, u32[]{:S(2)}) collective-permute-start(f32[286,2,2]{2,0,1:T(8,128)S(1)} %get-tuple-element.35), channel_id=1, source_target_pairs={{2,0},{4,2},{6,4},{0,6},{3,1},{5,3},{7,5},{1,7},{10,8},{12,10},{14... | collective-permute-start | bytes 13736 | tf_op jit(solution)/shard_map/ppermute | solution.py:46
  13.9 0.1 select_reduce_fusion
  14.0 0.6 reduce_sum.19
  14.6 1.2 %broadcast_divide_fusion = f32[512]{0:T(512)} fusion(f32[512]{0:T(512)S(1)} %reduce_prod.19, f32[]{:T(128)} %reduce_sum.19), kind=kLoop, calls=%fused_computation.109 | loop fusion | flops 512 | bytes 4100 | tf_op jit(solution)/shard_map/div | solution.py:37
  15.9 0.2 fusion.54
  16.1 3.4 %convolution_reduce_fusion = f32[286,512]{1,0:T(8,128)S(1)} fusion(f32[512,10,4]{0,2,1:T(4,128)S(1)} %fusion.54, s32[286,10]{0,1:T(8,128)} %param.11), kind=kOutput, calls=%fused_computation | convolution fusion | flops 71616688 | bytes 679088 | tf_op jit(solution)/shard_map/qdn,pdn->qpd/dot_general | solution.py:34
  19.5 1.4 %collective-permute-done.5 = f32[286,2,2]{2,0,1:T(8,128)S(1)} collective-permute-done((f32[286,2,2]{2,0,1:T(8,128)S(1)}, f32[286,2,2]{2,0,1:T(8,128)S(1)}, u32[]{:S(2)}, u32[]{:S(2)}) %collective-permute-start.5) | collective-permute-done | bytes 4608 | tf_op jit(solution)/shard_map/ppermute | solution.py:46
  20.9 7.3 %collective-permute-done.4 = f32[286,2,2]{2,0,1:T(8,128)S(1)} collective-permute-done((f32[286,2,2]{2,0,1:T(8,128)S(1)}, f32[286,2,2]{2,0,1:T(8,128)S(1)}, u32[]{:S(2)}, u32[]{:S(2)}) %collective-permute-start.4) | collective-permute-done | bytes 4608 | tf_op jit(solution)/shard_map/ppermute | solution.py:46
  28.3 1.2 %concatenate.47 = f32[286,776]{1,0:T(8,128)} concatenate(f32[286,128]{1,0:T(8,128)S(1)} %get-tuple-element.44, f32[286,128]{1,0:T(8,128)S(1)} %get-tuple-element.43, f32[286,128]{1,0:T(8,128)S(1)} %get-tuple-element.42, f32[286,128]{1,0:T(8,128)S(1)} %get-tuple-element.41, f32[286,128]{1,0:T(8,128)S(1)} %get-tuple-element.40, f32[286,128]{1,0:T(8,128)S(1)} %get-tuple-element.39, ...), dimensions={1} | concatenate | bytes 1775488 | tf_op jit(solution)/shard_map/concatenate | solution.py:72
  29.5 3.9 %fusion.65 = f32[512,776]{0,1:T(8,128)S(1)} fusion(f32[286,512]{1,0:T(8,128)S(1)} %convolution_reduce_fusion, f32[286,776]{1,0:T(8,128)} %concatenate.47), kind=kOutput, calls=%fused_computation.118 | convolution fusion | flops 1363574784 | bytes 3062720 | tf_op jit(solution)/shard_map/dot_general | solution.py:72
  33.5 1.4 %fusion.62 = (f32[512,2,1]{2,1,0:T(2,128)S(1)}, f32[512,2,1]{2,1,0:T(2,128)}) fusion(f32[512,2,128]{2,1,0:T(2,128)S(1)} %bitcast.66), kind=kLoop, calls=%fused_computation.115 | loop fusion | bytes 16384 | tf_op jit(solution)/shard_map/slice | solution.py:60
  34.9 1.2 %copy.97 = f32[512,2,1]{0,2,1:T(1,128)S(1)} copy(f32[512,2,1]{2,1,0:T(2,128)} %get-tuple-element.20) | data formatting | bytes 8192
  36.1 1.5 %collective-permute-start.1 = (f32[512,2,1]{0,2,1:T(1,128)S(1)}, f32[512,2,1]{0,2,1:T(1,128)S(1)}, u32[]{:S(2)}, u32[]{:S(2)}) collective-permute-start(f32[512,2,1]{0,2,1:T(1,128)S(1)} %copy.97), channel_id=1, source_target_pairs={{2,0},{4,2},{6,4},{0,6},{3,1},{5,3},{7,5},{1,7},{10,8},{12,10},{14... | collective-permute-start | bytes 12296 | tf_op jit(solution)/shard_map/ppermute | solution.py:46
  37.6 1.2 %fusion.61 = (f32[512,1,128]{2,1,0:T(1,128)}, f32[512,1,128]{2,1,0:T(1,128)}) fusion(f32[512,2,128]{2,1,0:T(2,128)S(1)} %bitcast.67), kind=kLoop, calls=%fused_computation.114 | loop fusion | bytes 1048576 | tf_op jit(solution)/shard_map/slice | solution.py:63
  38.7 1.1 %copy.96 = f32[512,1,128]{0,2,1:T(8,128)S(1)} copy(f32[512,1,128]{2,1,0:T(1,128)} %get-tuple-element.17) | data formatting | bytes 524288
  39.8 1.1 %copy.98 = f32[512,1,128]{0,2,1:T(8,128)S(1)} copy(f32[512,1,128]{2,1,0:T(1,128)} %get-tuple-element.18) | data formatting | bytes 524288
  41.0 3.5 %collective-permute-start.7 = (f32[512,128]{0,1:T(8,128)S(1)}, f32[512,128]{0,1:T(8,128)}, u32[]{:S(2)}, u32[]{:S(2)}) collective-permute-start(f32[512,128]{0,1:T(8,128)S(1)} %bitcast.68), channel_id=1, source_target_pairs={{1,0},{8,1},{9,8},{16,9},{17,16},{24,17},{25,24},{0,25},{3,2},{10,... | collective-permute-start | bytes 786440 | tf_op jit(solution)/shard_map/ppermute | solution.py:46
  44.5 0.2 copy.95
  44.7 0.6 collective-permute-start
  45.3 3.9 %collective-permute-done = f32[512,2,1]{0,2,1:T(1,128)S(1)} collective-permute-done((f32[512,2,1]{0,2,1:T(1,128)S(1)}, f32[512,2,1]{0,2,1:T(1,128)S(1)}, u32[]{:S(2)}, u32[]{:S(2)}) %collective-permute-start) | collective-permute-done | bytes 4128 | tf_op jit(solution)/shard_map/ppermute | solution.py:46
  49.2 0.1 fusion.19
  49.3 0.5 copy-done.13
  49.8 1.1 %fusion.51 = (f32[512,128]{0,1:T(8,128)S(1)}, f32[512,128]{0,1:T(8,128)S(1)}) fusion(f32[512,776]{0,1:T(8,128)S(1)} %copy-done.1, f32[512,130]{0,1:T(8,128)S(1)} %fusion.19, f32[512,128]{0,1:T(8,128)} %collective-permute-done.6, f32[]{:T(128)S(6)} %select_n.7, f32[512,1,128]{0,2,1:T(8,128)S(1)} %copy.98), kind=kLoop, calls=%fused_computation.70 | loop fusion | flops 720896 | bytes 2621444 | tf_op jit(solution)/shard_map/add | solution.py:83
  51.1 1.2 %fusion.44 = f32[512,128]{0,1:T(8,128)S(1)} fusion(f32[512,776]{0,1:T(8,128)S(1)} %copy-done.1, f32[512,130]{0,1:T(8,128)S(1)} %fusion.21, f32[512,128]{0,1:T(8,128)} %collective-permute-done.7, f32[]{:T(128)S(6)} %select_n.8, f32[512,1,128]{0,2,1:T(8,128)S(1)} %copy.96), kind=kLoop, calls=%fused_computation.60 | loop fusion | flops 720896 | bytes 2097156 | tf_op jit(solution)/shard_map/add | solution.py:83
  52.3 0.7 fusion.2
  53.0 0.2 reshape.17
  53.3 0.1 fusion.63
  53.4 0.1 collective-permute-start.11
  53.5 2.1 %collective-permute-start.9 = (f32[286,2,128]{2,0,1:T(8,128)S(1)}, f32[286,2,128]{2,0,1:T(8,128)S(1)}, u32[]{:S(2)}, u32[]{:S(2)}) collective-permute-start(f32[286,2,128]{2,0,1:T(8,128)S(1)} %fusion.15), channel_id=1, source_target_pairs={{1,0},{8,1},{9,8},{16,9},{17,16},{24,17},{25,24},{0,25},{3,2},{10,... | collective-permute-start | bytes 878600 | tf_op jit(solution)/shard_map/ppermute | solution.py:46
  55.7 1.5 %collective-permute-start.10 = (f32[286,2,2]{2,0,1:T(8,128)S(1)}, f32[286,2,2]{2,0,1:T(8,128)S(1)}, u32[]{:S(2)}, u32[]{:S(2)}) collective-permute-start(f32[286,2,2]{2,0,1:T(8,128)S(1)} %get-tuple-element.24), channel_id=1, source_target_pairs={{0,2},{2,4},{4,6},{6,0},{1,3},{3,5},{5,7},{7,1},{8,10},{10,12},{12... | collective-permute-start | bytes 13736 | tf_op jit(solution)/shard_map/ppermute | solution.py:46
  57.2 6.2 %collective-permute-done.11 = f32[286,2,2]{2,0,1:T(8,128)S(1)} collective-permute-done((f32[286,2,2]{2,0,1:T(8,128)S(1)}, f32[286,2,2]{2,0,1:T(8,128)S(1)}, u32[]{:S(2)}, u32[]{:S(2)}) %collective-permute-start.11) | collective-permute-done | bytes 4608 | tf_op jit(solution)/shard_map/ppermute | solution.py:46
  63.3 6.4 %collective-permute-done.10 = f32[286,2,2]{2,0,1:T(8,128)S(1)} collective-permute-done((f32[286,2,2]{2,0,1:T(8,128)S(1)}, f32[286,2,2]{2,0,1:T(8,128)S(1)}, u32[]{:S(2)}, u32[]{:S(2)}) %collective-permute-start.10) | collective-permute-done | bytes 4608 | tf_op jit(solution)/shard_map/ppermute | solution.py:46
  69.8 0.7 slice_bitcast_fusion.2
  70.5 0.7 slice_bitcast_fusion.4
  71.2 0.7 slice_bitcast_fusion.8
  71.9 1.4 %concatenate.54 = f32[286,776]{1,0:T(8,128)S(1)} concatenate(f32[286,128]{1,0:T(8,128)} %get-tuple-element.32, f32[286,128]{1,0:T(8,128)} %get-tuple-element.31, f32[286,128]{1,0:T(8,128)S(1)} %get-tuple-element.30, f32[286,128]{1,0:T(8,128)S(1)} %get-tuple-element.29, f32[286,128]{1,0:T(8,128)} %get-tuple-element.28, f32[286,128]{1,0:T(8,128)} %get-tuple-element.27, ...), dimensions={1} | concatenate | bytes 1775488 | tf_op jit(solution)/shard_map/concatenate | solution.py:72
  73.3 2.7 %fusion.66 = f32[512,776]{0,1:T(8,128)S(1)} fusion(f32[286,512]{1,0:T(8,128)S(1)} %convolution_reduce_fusion, f32[286,776]{1,0:T(8,128)S(1)} %concatenate.54), kind=kOutput, calls=%fused_computation.119 | convolution fusion | flops 1363574784 | bytes 3062720 | tf_op jit(solution)/shard_map/dot_general | solution.py:72
  76.2 1.1 %fusion.37 = (f32[512,128]{0,1:T(8,128)S(1)}, f32[512,128]{0,1:T(8,128)S(1)}) fusion(f32[512,776]{0,1:T(8,128)S(1)} %fusion.66, f32[512,130]{0,1:T(8,128)S(1)} %fusion.23, f32[512,128]{0,1:T(8,128)} %collective-permute-done.6, f32[]{:T(128)S(6)} %select_n.7, f32[512,1,128]{0,2,1:T(8,128)S(1)} %copy.98), kind=kLoop, calls=%fused_computation.50 | loop fusion | flops 720896 | bytes 2621444 | tf_op jit(solution)/shard_map/add | solution.py:83
  77.4 0.1 fusion.25
  77.5 1.1 %fusion.30 = f32[512,128]{0,1:T(8,128)S(1)} fusion(f32[512,776]{0,1:T(8,128)S(1)} %fusion.66, f32[512,130]{0,1:T(8,128)S(1)} %fusion.25, f32[512,128]{0,1:T(8,128)} %collective-permute-done.7, f32[]{:T(128)S(6)} %select_n.8, f32[512,1,128]{0,2,1:T(8,128)S(1)} %copy.96), kind=kLoop, calls=%fused_computation.40 | loop fusion | flops 720896 | bytes 2097156 | tf_op jit(solution)/shard_map/add | solution.py:83
  78.6 0.7 fusion
  79.3 0.2 reshape.18
  79.5 0.9 %copy.89 = f32[286,2,128]{2,1,0:T(2,128)} copy(f32[286,2,128]{2,0,1:T(8,128)S(1)} %fusion.12) | data formatting | bytes 585728 | tf_op jit(solution)/shard_map/add | solution.py:86
  (68 shorter events, 0.7 us)
Async XLA Ops:
  1.0 27.2 %collective-permute-start.3 = (f32[286,2,128]{2,0,1:T(8,128)S(1)}, f32[286,2,128]{2,0,1:T(8,128)S(1)}, u32[]{:S(2)}, u32[]{:S(2)}) collective-permute-start(f32[286,2,128]{2,0,1:T(8,128)S(1)} %copy.78), channel_id=1, source_target_pairs={{1,0},{8,1},{9,8},{16,9},{17,16},{24,17},{25,24},{0,25},{3,2},{10,... | collective-permute-start | bytes 878600 | tf_op jit(solution)/shard_map/ppermute | solution.py:46
  5.5 22.7 %collective-permute-start.2 = (f32[286,2,128]{2,0,1:T(8,128)S(1)}, f32[286,2,128]{2,0,1:T(8,128)S(1)}, u32[]{:S(2)}, u32[]{:S(2)}) collective-permute-start(f32[286,2,128]{2,0,1:T(8,128)S(1)} %copy.78), channel_id=1, source_target_pairs={{0,1},{1,8},{8,9},{9,16},{16,17},{17,24},{24,25},{25,0},{2,3},{3,1... | collective-permute-start | bytes 878600 | tf_op jit(solution)/shard_map/ppermute | solution.py:46
  7.6 6.3 %copy-start.4 = (s32[512,10]{0,1:T(8,128)S(1)}, s32[512,10]{0,1:T(8,128)}, u32[]{:S(2)}) copy-start(s32[512,10]{0,1:T(8,128)} %param.10) | copy-start | bytes 61444
  7.6 6.3 %copy-start.16 = (f32[4]{0:T(128)S(1)}, f32[4]{0:T(128)}, u32[]{:S(2)}) copy-start(f32[4]{0:T(128)} %constant.42.clone) | copy-start | bytes 52
  7.6 8.3 %copy-start.15 = (f32[4,4,1]{1,0,2:T(4,128)S(1)}, f32[4,4,1]{1,0,2:T(4,128)}, u32[]{:S(2)}) copy-start(f32[4,4,1]{1,0,2:T(4,128)} %constant.56) | copy-start | bytes 196
  7.6 25.9 %all-to-all-start = ((f32[128,4,2,128]{3,2,0,1:T(2,128)}), f32[128,4,2,128]{3,2,0,1:T(2,128)S(1)}, u32[]{:S(2)}, u32[]{:S(2)}) async-start(f32[128,4,2,128]{3,2,0,1:T(2,128)} %copy.67), calls=%async_computation | async-start | bytes 1048576 | tf_op jit(solution)/shard_map/all_to_all | solution.py:57
  11.3 9.5 %collective-permute-start.5 = (f32[286,2,2]{2,0,1:T(8,128)S(1)}, f32[286,2,2]{2,0,1:T(8,128)S(1)}, u32[]{:S(2)}, u32[]{:S(2)}) collective-permute-start(f32[286,2,2]{2,0,1:T(8,128)S(1)} %get-tuple-element.35), channel_id=1, source_target_pairs={{2,0},{4,2},{6,4},{0,6},{3,1},{5,3},{7,5},{1,7},{10,8},{12,10},{14... | collective-permute-start | bytes 13736 | tf_op jit(solution)/shard_map/ppermute | solution.py:46
  13.8 14.3 %collective-permute-start.4 = (f32[286,2,2]{2,0,1:T(8,128)S(1)}, f32[286,2,2]{2,0,1:T(8,128)S(1)}, u32[]{:S(2)}, u32[]{:S(2)}) collective-permute-start(f32[286,2,2]{2,0,1:T(8,128)S(1)} %get-tuple-element.36), channel_id=1, source_target_pairs={{0,2},{2,4},{4,6},{6,0},{1,3},{3,5},{5,7},{7,1},{8,10},{10,12},{12... | collective-permute-start | bytes 13736 | tf_op jit(solution)/shard_map/ppermute | solution.py:46
  33.5 2.6 %copy-start = (f32[512,776]{0,1:T(8,128)}, f32[512,776]{0,1:T(8,128)S(1)}, u32[]{:S(2)}) copy-start(f32[512,776]{0,1:T(8,128)S(1)} %fusion.65) | copy-start | bytes 4767748
  36.1 9.2 %collective-permute-start.1 = (f32[512,2,1]{0,2,1:T(1,128)S(1)}, f32[512,2,1]{0,2,1:T(1,128)S(1)}, u32[]{:S(2)}, u32[]{:S(2)}) collective-permute-start(f32[512,2,1]{0,2,1:T(1,128)S(1)} %copy.97), channel_id=1, source_target_pairs={{2,0},{4,2},{6,4},{0,6},{3,1},{5,3},{7,5},{1,7},{10,8},{12,10},{14... | collective-permute-start | bytes 12296 | tf_op jit(solution)/shard_map/ppermute | solution.py:46
  37.6 11.7 %slice-start = ((f32[512,776]{0,1:T(8,128)}), f32[512,128]{0,1:T(8,128)S(1)}, s32[]{:S(2)}) async-start(f32[512,776]{0,1:T(8,128)} %copy-done), calls=%async_computation.1 | async-start | bytes 524288 | tf_op jit(solution)/shard_map/slice | solution.py:73
  37.6 12.3 %copy-start.1 = (f32[512,776]{0,1:T(8,128)S(1)}, f32[512,776]{0,1:T(8,128)}, u32[]{:S(2)}) copy-start(f32[512,776]{0,1:T(8,128)} %copy-done) | copy-start | bytes 4767748
  40.9 8.9 %collective-permute-start.6 = (f32[512,128]{0,1:T(8,128)S(1)}, f32[512,128]{0,1:T(8,128)}, u32[]{:S(2)}, u32[]{:S(2)}) collective-permute-start(f32[512,128]{0,1:T(8,128)S(1)} %bitcast.71), channel_id=1, source_target_pairs={{0,1},{1,8},{8,9},{9,16},{16,17},{17,24},{24,25},{25,0},{2,3},{3,1... | collective-permute-start | bytes 786440 | tf_op jit(solution)/shard_map/ppermute | solution.py:46
  41.0 10.1 %collective-permute-start.7 = (f32[512,128]{0,1:T(8,128)S(1)}, f32[512,128]{0,1:T(8,128)}, u32[]{:S(2)}, u32[]{:S(2)}) collective-permute-start(f32[512,128]{0,1:T(8,128)S(1)} %bitcast.68), channel_id=1, source_target_pairs={{1,0},{8,1},{9,8},{16,9},{17,16},{24,17},{25,24},{0,25},{3,2},{10,... | collective-permute-start | bytes 786440 | tf_op jit(solution)/shard_map/ppermute | solution.py:46
  44.7 4.5 %collective-permute-start = (f32[512,2,1]{0,2,1:T(1,128)S(1)}, f32[512,2,1]{0,2,1:T(1,128)S(1)}, u32[]{:S(2)}, u32[]{:S(2)}) collective-permute-start(f32[512,2,1]{0,2,1:T(1,128)S(1)} %copy.95), channel_id=1, source_target_pairs={{0,2},{2,4},{4,6},{6,0},{1,3},{3,5},{5,7},{7,1},{8,10},{10,12},{12... | collective-permute-start | bytes 12296 | tf_op jit(solution)/shard_map/ppermute | solution.py:46
  45.3 4.0 %copy-start.11 = (f32[512,1]{0,1:T(1,128)}, f32[512,1]{0,1:T(1,128)S(1)}, u32[]{:S(2)}) copy-start(f32[512,1]{0,1:T(1,128)S(1)} %get-tuple-element.47) | copy-start | bytes 6148
  45.3 5.7 %copy-start.7 = (f32[512,1]{0,1:T(1,128)}, f32[512,1]{0,1:T(1,128)S(1)}, u32[]{:S(2)}) copy-start(f32[512,1]{0,1:T(1,128)S(1)} %get-tuple-element.48) | copy-start | bytes 6148
  49.2 0.6 copy-start.13
  49.2 1.8 %copy-start.9 = (f32[512,1]{0,1:T(1,128)}, f32[512,1]{0,1:T(1,128)S(1)}, u32[]{:S(2)}) copy-start(f32[512,1]{0,1:T(1,128)S(1)} %get-tuple-element.46) | copy-start | bytes 6148
  51.0 1.3 %copy-start.5 = (f32[512]{0:T(512)S(1)}, f32[512]{0:T(512)}, u32[]{:S(2)}) copy-start(f32[512]{0:T(512)} %broadcast_divide_fusion) | copy-start | bytes 6148
  51.1 2.1 %copy-start.2 = (f32[286,2,128]{2,1,0:T(2,128)S(1)}, f32[286,2,128]{2,1,0:T(2,128)}, u32[]{:S(2)}) copy-start(f32[286,2,128]{2,1,0:T(2,128)} %param.7) | copy-start | bytes 878596
  51.1 2.1 %copy-start.3 = (f32[286,2,128]{2,1,0:T(2,128)S(1)}, f32[286,2,128]{2,1,0:T(2,128)}, u32[]{:S(2)}) copy-start(f32[286,2,128]{2,1,0:T(2,128)} %param.8) | copy-start | bytes 878596
  53.4 9.9 %collective-permute-start.11 = (f32[286,2,2]{2,0,1:T(8,128)S(1)}, f32[286,2,2]{2,0,1:T(8,128)S(1)}, u32[]{:S(2)}, u32[]{:S(2)}) collective-permute-start(f32[286,2,2]{2,0,1:T(8,128)S(1)} %get-tuple-element.23), channel_id=1, source_target_pairs={{2,0},{4,2},{6,4},{0,6},{3,1},{5,3},{7,5},{1,7},{10,8},{12,10},{14... | collective-permute-start | bytes 13736 | tf_op jit(solution)/shard_map/ppermute | solution.py:46
  53.5 16.9 %collective-permute-start.9 = (f32[286,2,128]{2,0,1:T(8,128)S(1)}, f32[286,2,128]{2,0,1:T(8,128)S(1)}, u32[]{:S(2)}, u32[]{:S(2)}) collective-permute-start(f32[286,2,128]{2,0,1:T(8,128)S(1)} %fusion.15), channel_id=1, source_target_pairs={{1,0},{8,1},{9,8},{16,9},{17,16},{24,17},{25,24},{0,25},{3,2},{10,... | collective-permute-start | bytes 878600 | tf_op jit(solution)/shard_map/ppermute | solution.py:46
  55.7 15.5 %collective-permute-start.8 = (f32[286,2,128]{2,0,1:T(8,128)S(1)}, f32[286,2,128]{2,0,1:T(8,128)S(1)}, u32[]{:S(2)}, u32[]{:S(2)}) collective-permute-start(f32[286,2,128]{2,0,1:T(8,128)S(1)} %fusion.15), channel_id=1, source_target_pairs={{0,1},{1,8},{8,9},{9,16},{16,17},{17,24},{24,25},{25,0},{2,3},{3,1... | collective-permute-start | bytes 878600 | tf_op jit(solution)/shard_map/ppermute | solution.py:46
  55.7 14.1 %collective-permute-start.10 = (f32[286,2,2]{2,0,1:T(8,128)S(1)}, f32[286,2,2]{2,0,1:T(8,128)S(1)}, u32[]{:S(2)}, u32[]{:S(2)}) collective-permute-start(f32[286,2,2]{2,0,1:T(8,128)S(1)} %get-tuple-element.24), channel_id=1, source_target_pairs={{0,2},{2,4},{4,6},{6,0},{1,3},{3,5},{5,7},{7,1},{8,10},{10,12},{12... | collective-permute-start | bytes 13736 | tf_op jit(solution)/shard_map/ppermute | solution.py:46
  73.3 2.8 %copy-start.12 = (f32[512,1]{0,1:T(1,128)S(1)}, f32[512,1]{0,1:T(1,128)}, u32[]{:S(2)}) copy-start(f32[512,1]{0,1:T(1,128)} %copy-done.11) | copy-start | bytes 6148
  73.3 2.8 %copy-start.14 = (f32[512,1]{0,1:T(1,128)S(1)}, f32[512,1]{0,1:T(1,128)}, u32[]{:S(2)}) copy-start(f32[512,1]{0,1:T(1,128)} %copy-done.13) | copy-start | bytes 6148
  76.1 1.3 %copy-start.8 = (f32[512,1]{0,1:T(1,128)S(1)}, f32[512,1]{0,1:T(1,128)}, u32[]{:S(2)}) copy-start(f32[512,1]{0,1:T(1,128)} %copy-done.7) | copy-start | bytes 6148
  76.1 1.3 %copy-start.10 = (f32[512,1]{0,1:T(1,128)S(1)}, f32[512,1]{0,1:T(1,128)}, u32[]{:S(2)}) copy-start(f32[512,1]{0,1:T(1,128)} %copy-done.9) | copy-start | bytes 6148
  77.4 1.2 %copy-start.6 = (f32[512]{0:T(512)S(1)}, f32[512]{0:T(512)}, u32[]{:S(2)}) copy-start(f32[512]{0:T(512)} %broadcast_divide_fusion) | copy-start | bytes 6148

commit v2 on v1

v2 whole, which is shorter than its diff:
```python
import functools
import math

import jax
import jax.numpy as jnp
from jax import lax
from jax.experimental import pallas as pl
from jax.experimental.pallas import tpu as pltpu
from jax.sharding import PartitionSpec as P

STEPS = 2
SUB = 32

gauss_nodes = (-2.3344142183389773, -0.7419637843027259, 0.7419637843027259, 2.3344142183389773)
gauss_weights = (0.04587585476806849, 0.4541241452319315, 0.4541241452319315, 0.04587585476806849)
mass_shift = 1.0
relax_rate = 0.2
f32 = jnp.float32
bf16 = jnp.bfloat16


def split(x):
    high = x.astype(bf16)
    return high, (x - high.astype(f32)).astype(bf16)


def dot3(ah, al, bh, bl):
    dot = functools.partial(jnp.dot, preferred_element_type=f32)
    return dot(ah, bh) + (dot(ah, bl) + dot(al, bh))


def kernel(
    dims, lam_ref, adj_ref, coef_ref, quad_ref, mode_ref, out_ref,
    kfull, kedge, ksend, krecv, vhalo, vsend, vrecv, lam1, u,
    psi, psi_h, psi_l, bt_h, bt_l, d_h, d_l,
    main_send, main_recv, fwd_send, fwd_recv, v_send, v_recv,
):
    n, ncore, ngx, inputs, modes, rows_p, wide, points, pts = dims
    z, x, c = lax.axis_index("chaos"), lax.axis_index("gx"), lax.axis_index("gy")
    count = n * ncore
    me = z * ncore + c
    above = lax.rem(me + 1, count)
    below = lax.rem(me + count - 1, count)
    has_above, has_below = me < count - 1, me > 0
    dev_above = {"chaos": lax.div(above, ncore), "gy": lax.rem(above, ncore)}
    dev_below = {"chaos": lax.div(below, ncore), "gy": lax.rem(below, ncore)}
    dev_right = {"gx": lax.rem(x + 1, ngx)}
    dev_left = {"gx": lax.rem(x + ngx - 1, ngx)}

    def remote(src, dst, ss, rs, dev):
        return pltpu.make_async_remote_copy(
            src_ref=src, dst_ref=dst, send_sem=ss, recv_sem=rs, device_id=dev,
            device_id_type=pl.DeviceIdType.MESH,
        )

    barrier = pltpu.get_barrier_semaphore()

    def greet(dev):
        pl.semaphore_signal(barrier, inc=1, device_id=dev, device_id_type=pl.DeviceIdType.MESH)

    for d in range(1, n):
        greet({"chaos": lax.rem(z + d, n)})
    greet(dev_left)
    greet(dev_right)

    greet(dev_above)
    greet(dev_below)
    pl.semaphore_wait(barrier, n + 3)

    def main_copy(to):
        return remote(coef_ref.at[to], kfull.at[z, pl.ds(1, 2)], main_send.at[to], main_recv.at[z], {"chaos": to})

    def v_copies(step, src):
        return (
            remote(src, vhalo.at[step, 0], v_send.at[step, 0], v_recv.at[step, 0], dev_above),
            remote(src, vhalo.at[step, 1], v_send.at[step, 1], v_recv.at[step, 1], dev_below),
            remote(vsend.at[step, 0], vrecv.at[step, 1], v_send.at[step, 2], v_recv.at[step, 2], dev_left),
            remote(vsend.at[step, 1], vrecv.at[step, 0], v_send.at[step, 3], v_recv.at[step, 3], dev_right),
        )

    def start_v(step, src):
        up, down, left, right = v_copies(step, src)

        @pl.when(has_above)
        def _():
            up.start()

        @pl.when(has_below)
        def _():
            down.start()

        for r in range(2):
            flipped = jnp.concatenate([src[r], jnp.zeros((wide - rows_p, 128), f32)], 0).T
            vsend[step, 0, r] = flipped[:8]
            vsend[step, 1, r] = flipped[120:]
        left.start()
        right.start()

    def fwd_copies(j):
        return (
            remote(kfull.at[j, 2], kfull.at[j, 0], fwd_send.at[0, j], fwd_recv.at[0, j], dev_above),
            remote(kfull.at[j, 1], kfull.at[j, 3], fwd_send.at[1, j], fwd_recv.at[1, j], dev_below),
            remote(ksend.at[j, 0], krecv.at[j, 1], fwd_send.at[2, j], fwd_recv.at[2, j], dev_left),
            remote(ksend.at[j, 1], krecv.at[j, 0], fwd_send.at[3, j], fwd_recv.at[3, j], dev_right),
        )

    def forward(j):
        up, down, left, right = fwd_copies(j)

        @pl.when(has_above)
        def _():
            up.start()

        @pl.when(has_below)
        def _():
            down.start()

        for r in range(2):
            flipped = kfull[j, 1 + r].T
            ksend[j, 0, r] = flipped[:8]
            ksend[j, 1, r] = flipped[120:]
        left.start()
        right.start()

    for d in range(1, n):
        main_copy(lax.rem(z + d, n)).start()
    start_v(0, lam_ref)
    kfull[z, pl.ds(1, 2)] = coef_ref[z]
    forward(z)

    @pl.when(jnp.logical_not(has_below))
    def _():
        kfull[:, 0] = jnp.zeros((n, pts, 128), f32)
        vhalo[:, 0] = jnp.zeros((STEPS, 2, rows_p, 128), f32)

    @pl.when(jnp.logical_not(has_above))
    def _():
        kfull[:, 3] = jnp.zeros((n, pts, 128), f32)
        vhalo[:, 1] = jnp.zeros((STEPS, 2, rows_p, 128), f32)

    lane = lax.broadcasted_iota(jnp.int32, (1, 128), 1)
    quad = quad_ref[...]
    wts = jnp.where((quad == 0) | (quad == 3), gauss_weights[0], gauss_weights[1]).astype(f32)
    wts = jnp.where(lane < inputs, wts, 1.0)
    shift = 8
    while shift:
        wts = wts * pltpu.roll(wts, 128 - shift, 1)
        shift //= 2
    wts = wts[:, :1]
    wts = wts / jnp.sum(wts, axis=0, keepdims=True) * 0.25
    keep = jnp.where(lax.broadcasted_iota(jnp.int32, (SUB, wide), 1) < modes, 1.0, 0.0).astype(f32)

    def basis(i, carry):
        rows = pl.ds(pl.multiple_of(i * SUB, SUB), SUB)
        q = quad_ref[rows, :]
        node = jnp.where(
            q == 0, gauss_nodes[0], jnp.where(q == 1, gauss_nodes[1], jnp.where(q == 2, gauss_nodes[2], gauss_nodes[3]))
        ).astype(f32)
        h2 = (node * node - 1.0) * (1.0 / math.sqrt(2.0))
        h3 = (node * node * node - 3.0 * node) * (1.0 / math.sqrt(6.0))
        total = keep
        for d in range(inputs):
            deg = mode_ref[d : d + 1, :]
            total = total * jnp.where(
                deg == 0,
                1.0,
                jnp.where(deg == 1, node[:, d : d + 1], jnp.where(deg == 2, h2[:, d : d + 1], h3[:, d : d + 1])),
            )
        psi[rows, :] = total
        high, low = split(total)
        psi_h[rows, :] = high
        psi_l[rows, :] = low
        return carry

    lax.fori_loop(0, points // SUB, basis, 0)
    for i in range(points // 128):
        part = slice(i * 128, i * 128 + 128)
        flipped = (psi[part, :] * wts[part]).T[:rows_p]
        high, low = split(flipped)
        bt_h[:, part] = high
        bt_l[:, part] = low

    def to_points(at, first, second):
        vh, vl = split(jnp.concatenate([first, second], 1))
        res = dot3(psi_h[:, :rows_p], psi_l[:, :rows_p], vh, vl)
        u[at] = res[:, :128]
        u[at + 1] = res[:, 128:]

    def fields(step, src):
        to_points(2, src[0], src[1])
        up, down, left, right = v_copies(step, src)

        @pl.when(has_below)
        def _():
            up.wait_recv()

        to_points(0, vhalo[step, 0, 0], vhalo[step, 0, 1])

        @pl.when(has_above)
        def _():
            down.wait_recv()

        to_points(4, vhalo[step, 1, 0], vhalo[step, 1, 1])
        left.wait_recv()
        right.wait_recv()
        edge = [
            jnp.concatenate([vrecv[step, 1, r], jnp.zeros((112, wide), f32), vrecv[step, 0, r]], 0).T[:rows_p]
            for r in range(2)
        ]
        to_points(6, edge[0], edge[1])

    is_first, is_last = lane == 0, lane == 127

    def stencil(i, carry):
        rows = pl.ds(pl.multiple_of(i * SUB, SUB), SUB)
        per = pts // SUB
        j = lax.div(i, per)
        sub = pl.ds(pl.multiple_of(lax.rem(i, per) * SUB, SUB), SUB)
        uy = [u[k, rows, :] for k in range(8)]
        ky = [kfull[j, k, sub, :] for k in range(4)]
        fy = [ky[k] * (uy[k + 2] - uy[k]) for k in range(4)]
        for r in range(2):
            mid, end = uy[2 + r], uy[6 + r]
            a, b = pltpu.roll(mid, 127, 1), pltpu.roll(end, 127, 1)
            e, f = pltpu.roll(mid, 1, 1), pltpu.roll(end, 1, 1)
            fx = ky[1 + r] * (jnp.where(is_last, b, a) - jnp.where(is_first, f, e))
            fe = kedge[j, r, sub, :] * (jnp.where(is_last, a, b) - jnp.where(is_first, e, f))
            nxt = jnp.where(is_last, pltpu.roll(fe, 127, 1), pltpu.roll(fx, 127, 1))
            prv = jnp.where(is_first, pltpu.roll(fe, 1, 1), pltpu.roll(fx, 1, 1))
            high, low = split((nxt - prv) + (fy[r + 2] - fy[r]))
            d_h[rows, r * 128 : r * 128 + 128] = high
            d_l[rows, r * 128 : r * 128 + 128] = low
        return carry

    def update(src, dst):
        lax.fori_loop(0, points // SUB, stencil, 0)
        div = dot3(bt_h[...], bt_l[...], d_h[...], d_l[...])
        for r in range(2):
            v = src[r]
            dst[r] = v + relax_rate * (adj_ref[r] - (mass_shift * v - div[:, r * 128 : r * 128 + 128]))

    for d in range(1, n):
        j = lax.rem(z + d, n)
        remote(coef_ref.at[j], kfull.at[j, pl.ds(1, 2)], main_send.at[j], main_recv.at[j], {"chaos": j}).wait_recv()
        forward(j)
    fields(0, lam_ref)

    def arrive(j, carry):
        up, down, left, right = fwd_copies(j)

        @pl.when(has_below)
        def _():
            up.wait_recv()

        @pl.when(has_above)
        def _():
            down.wait_recv()

        left.wait_recv()
        right.wait_recv()
        for r in range(2):
            kedge[j, r] = jnp.concatenate([krecv[j, 1, r], jnp.zeros((112, pts), f32), krecv[j, 0, r]], 0).T
        return carry

    lax.fori_loop(0, n, arrive, 0)
    update(lam_ref, lam1)
    start_v(1, lam1)
    fields(1, lam1)
    update(lam1, out_ref)

    for d in range(1, n):
        main_copy(lax.rem(z + d, n)).wait_send()

    def drain(copies):
        up, down, left, right = copies

        @pl.when(has_above)
        def _():
            up.wait_send()

        @pl.when(has_below)
        def _():
            down.wait_send()

        left.wait_send()
        right.wait_send()

    def drain_one(j, carry):
        drain(fwd_copies(j))
        return carry

    lax.fori_loop(0, n, drain_one, 0)
    drain(v_copies(0, lam_ref))
    drain(v_copies(1, lam1))


def local(mesh_sizes, lam_start, adj_source, coef_points, quad_index, mode_index):
    n, ngx, ncore = mesh_sizes
    modes = lam_start.shape[0]
    points, inputs = quad_index.shape
    pts = coef_points.shape[0]
    rows_p = -(-modes // 16) * 16
    wide = -(-modes // 128) * 128
    dims = (n, ncore, ngx, inputs, modes, rows_p, wide, points, pts)

    def by_row(v):
        return jnp.pad(jnp.transpose(v, (1, 0, 2)), ((0, 0), (0, rows_p - modes), (0, 0)))

    coef = jnp.transpose(coef_points, (1, 2, 0, 3))
    quad = jnp.pad(quad_index, ((0, 0), (0, 128 - inputs)))
    mode = jnp.pad(mode_index.T, ((0, 16 - inputs), (0, wide - modes)))
    vmem = pl.BlockSpec(memory_space=pltpu.VMEM)
    dma = pltpu.SemaphoreType.DMA
    out = pl.pallas_call(
        functools.partial(kernel, dims),
        out_shape=jax.ShapeDtypeStruct((2, rows_p, 128), f32),
        in_specs=[vmem] * 5,
        out_specs=vmem,
        scratch_shapes=[
            pltpu.VMEM((n, 4, pts, 128), f32),
            pltpu.VMEM((n, 2, pts, 128), f32),
            pltpu.VMEM((n, 2, 2, 8, pts), f32),
            pltpu.VMEM((n, 2, 2, 8, pts), f32),
            pltpu.VMEM((STEPS, 2, 2, rows_p, 128), f32),
            pltpu.VMEM((STEPS, 2, 2, 8, wide), f32),
            pltpu.VMEM((STEPS, 2, 2, 8, wide), f32),
            pltpu.VMEM((2, rows_p, 128), f32),
            pltpu.VMEM((8, points, 128), f32),
            pltpu.VMEM((points, wide), f32),
            pltpu.VMEM((points, wide), bf16),
            pltpu.VMEM((points, wide), bf16),
            pltpu.VMEM((rows_p, points), bf16),
            pltpu.VMEM((rows_p, points), bf16),
            pltpu.VMEM((points, 256), bf16),
            pltpu.VMEM((points, 256), bf16),
            dma((n,)), dma((n,)), dma((4, n)), dma((4, n)), dma((STEPS, 4)), dma((STEPS, 4)),
        ],
        compiler_params=pltpu.CompilerParams(
            collective_id=0, has_side_effects=True, vmem_limit_bytes=40 * 1024 * 1024
        ),
    )(by_row(lam_start), by_row(adj_source), coef, quad, mode)
    return jnp.transpose(out[:, :modes], (1, 0, 2))


def solution(mesh):
    sizes = (mesh.shape["chaos"], mesh.shape["gx"], mesh.shape["gy"])
    placed = (
        P(None, ("chaos", "gy"), "gx"),
        P(None, ("chaos", "gy"), "gx"),
        P("chaos", None, "gy", "gx"),
        P(),
        P(),
    )
    return jax.shard_map(
        functools.partial(local, sizes),
        mesh=mesh,
        in_specs=placed,
        out_specs=P(None, ("chaos", "gy"), "gx"),
        check_vma=False,
    )
```

time: 81.1 us -> 42.7 us (0.53)
  the two profiles are of different devices: /device:TPU:0 before, /device:TPU:9 now
where the time goes in v2:
time: 42.7 us; the launch traced here: 42.4 us
  Pallas kernels  37.4 us (88%)
  local copies, waits for them, and re-layouts  4.92 us (12%)
    pallas_call x1, Pallas kernels, local(): pl.pallas_call(functools.partial(kernel, dims), out_shape=jax.ShapeDtypeS...  37.4 us
    unnamed x12, local copies, waits for them, and re-layouts  3.15 us
    transpose x2, local copies, waits for them, and re-layouts, local(): return jnp.transpose(out[:, :modes], (1, 0, 2))  0.96 us

profile of v2, /device:TPU:9, one launch (start us, length us, event | category | flops | bytes accessed | tf_op | source)
XLA Modules:
  0.0 42.4 jit_solution(3527719663295090475)
XLA Ops:
  0.0 0.0 copy-start.3
  0.0 0.7 %pad.18.mode_ref = s32[16,384]{1,0:T(8,128)S(1)} pad(s32[10,286]{1,0:T(8,128)} %bitcast.15, s32[]{:T(128)} %constant.3.clone.1), padding=0_6x0_98 | pad | bytes 36020 | tf_op jit(solution)/shard_map/jit(_pad)/pad | solution.py:311
  0.8 0.0 copy-done.3
  0.8 0.1 copy.9
  0.9 0.0 copy-start.1
  1.0 0.9 %copy-done.1 = f32[286,2,128]{2,1,0:T(2,128)S(1)} copy-done((f32[286,2,128]{2,1,0:T(2,128)S(1)}, f32[286,2,128]{2,1,0:T(2,128)}, u32[]{:S(2)}) %copy-start.1) | copy-done | bytes 292888
  1.9 0.0 copy-start.2
  2.0 0.9 %copy-done.2 = f32[286,2,128]{2,1,0:T(2,128)S(1)} copy-done((f32[286,2,128]{2,1,0:T(2,128)S(1)}, f32[286,2,128]{2,1,0:T(2,128)}, u32[]{:S(2)}) %copy-start.2) | copy-done | bytes 292888
  2.9 0.0 copy-start
  2.9 1.0 %copy-done = f32[128,4,2,128]{3,2,1,0:T(2,128)S(1)} copy-done((f32[128,4,2,128]{3,2,1,0:T(2,128)S(1)}, f32[128,4,2,128]{3,2,1,0:T(2,128)}, u32[]{:S(2)}) %copy-start) | copy-done | bytes 524312
  3.9 0.1 copy.14
  4.0 37.4 %shard_map.55 = f32[2,288,128]{2,1,0:T(8,128)S(1)} custom-call(f32[2,288,128]{2,1,0:T(8,128)S(1)} %pad.15.lam_ref, f32[2,288,128]{2,1,0:T(8,128)S(1)} %pad.16.adj_ref, f32[4,2,128,128]{3,2,1,0:T(8,128)S(1)} %bitcast.12, s32[512,128]{1,0:T(8,128)S(1)} %pad.17.quad_ref, s32[16,384]{1,0:T(8,128)S(1)} %pad.18.mode_ref), custom_call_target="tpu_custom_call" | custom-call | tf_op jit(solution)/shard_map/pallas_call | solution.py:314
  41.5 0.9 %copy.10 = f32[286,2,128]{2,1,0:T(2,128)} copy(f32[286,2,128]{2,0,1:T(8,128)S(1)} %slice_bitcast_fusion) | data formatting | bytes 585728 | tf_op jit(solution)/shard_map/transpose | solution.py:342
  (6 shorter events, 0.1 us)
Async XLA Ops:
  0.0 0.8 %copy-start.3 = (s32[512,10]{0,1:T(8,128)S(1)}, s32[512,10]{0,1:T(8,128)}, u32[]{:S(2)}) copy-start(s32[512,10]{0,1:T(8,128)} %param.8) | copy-start | bytes 61444
  0.9 1.0 %copy-start.1 = (f32[286,2,128]{2,1,0:T(2,128)S(1)}, f32[286,2,128]{2,1,0:T(2,128)}, u32[]{:S(2)}) copy-start(f32[286,2,128]{2,1,0:T(2,128)} %param.5) | copy-start | bytes 878596
  1.9 1.0 %copy-start.2 = (f32[286,2,128]{2,1,0:T(2,128)S(1)}, f32[286,2,128]{2,1,0:T(2,128)}, u32[]{:S(2)}) copy-start(f32[286,2,128]{2,1,0:T(2,128)} %param.6) | copy-start | bytes 878596
  2.9 1.0 %copy-start = (f32[128,4,2,128]{3,2,1,0:T(2,128)S(1)}, f32[128,4,2,128]{3,2,1,0:T(2,128)}, u32[]{:S(2)}) copy-start(f32[128,4,2,128]{3,2,1,0:T(2,128)} %param.7) | copy-start | bytes 1572868

commit v3 on v2

--- a/solution.py
+++ b/solution.py
@@ -10,6 +10,7 @@
 
 STEPS = 2
 SUB = 32
+TILE = 128
 
 gauss_nodes = (-2.3344142183389773, -0.7419637843027259, 0.7419637843027259, 2.3344142183389773)
 gauss_weights = (0.04587585476806849, 0.4541241452319315, 0.4541241452319315, 0.04587585476806849)
@@ -30,9 +31,9 @@
 
 
 def kernel(
-    dims, lam_ref, adj_ref, coef_ref, quad_ref, mode_ref, out_ref,
-    kfull, kedge, ksend, krecv, vhalo, vsend, vrecv, lam1, u,
-    psi, psi_h, psi_l, bt_h, bt_l, d_h, d_l,
+    dims, lam_raw, adj_hbm, coef_ref, quad_ref, mode_raw, out_ref,
+    adj_ref, in_sem, lam_ref, mode_ref,    kfull, kedge, ksend, krecv, vhalo, vsend, vrecv, lam1, u,
+    psi, psi_h, psi_l, bt_h, bt_l, d_h, d_l, d_x,
     main_send, main_recv, fwd_send, fwd_recv, v_send, v_recv,
 ):
     n, ncore, ngx, inputs, modes, rows_p, wide, points, pts = dims
@@ -53,6 +54,8 @@
             device_id_type=pl.DeviceIdType.MESH,
         )
 
+    fetch = pltpu.make_async_copy(adj_hbm, adj_ref, in_sem)
+    fetch.start()
     barrier = pltpu.get_barrier_semaphore()
 
     def greet(dev):
@@ -124,6 +127,9 @@
 
     for d in range(1, n):
         main_copy(lax.rem(z + d, n)).start()
+    for r in range(2):
+        lam_ref[r, :modes] = lam_raw[:, r, :]
+        lam_ref[r, modes:] = jnp.zeros((rows_p - modes, 128), f32)
     start_v(0, lam_ref)
     kfull[z, pl.ds(1, 2)] = coef_ref[z]
     forward(z)
@@ -140,13 +146,12 @@
 
     lane = lax.broadcasted_iota(jnp.int32, (1, 128), 1)
     quad = quad_ref[...]
-    wts = jnp.where((quad == 0) | (quad == 3), gauss_weights[0], gauss_weights[1]).astype(f32)
-    wts = jnp.where(lane < inputs, wts, 1.0)
-    shift = 8
-    while shift:
-        wts = wts * pltpu.roll(wts, 128 - shift, 1)
-        shift //= 2
-    wts = wts[:, :1]
+    each = jnp.where((quad == 0) | (quad == 3), gauss_weights[0], gauss_weights[1]).astype(f32)
+    wts = each[:, :1]
+    for d in range(1, inputs):
+        wts = wts * each[:, d : d + 1]
+    mode_ref[...] = jnp.zeros((16, wide), f32)
+    mode_ref[:inputs, :modes] = mode_raw[...].astype(f32)
     wts = wts / jnp.sum(wts, axis=0, keepdims=True) * 0.25
     keep = jnp.where(lax.broadcasted_iota(jnp.int32, (SUB, wide), 1) < modes, 1.0, 0.0).astype(f32)
 
@@ -162,9 +167,9 @@
         for d in range(inputs):
             deg = mode_ref[d : d + 1, :]
             total = total * jnp.where(
-                deg == 0,
+                deg == 0.0,
                 1.0,
-                jnp.where(deg == 1, node[:, d : d + 1], jnp.where(deg == 2, h2[:, d : d + 1], h3[:, d : d + 1])),
+                jnp.where(deg == 1.0, node[:, d : d + 1], jnp.where(deg == 2.0, h2[:, d : d + 1], h3[:, d : d + 1])),
             )
         psi[rows, :] = total
         high, low = split(total)
@@ -186,21 +191,11 @@
         u[at] = res[:, :128]
         u[at + 1] = res[:, 128:]
 
-    def fields(step, src):
+    def own(src):
         to_points(2, src[0], src[1])
-        up, down, left, right = v_copies(step, src)
-
-        @pl.when(has_below)
-        def _():
-            up.wait_recv()
-
-        to_points(0, vhalo[step, 0, 0], vhalo[step, 0, 1])
-
-        @pl.when(has_above)
-        def _():
-            down.wait_recv()
-
-        to_points(4, vhalo[step, 1, 0], vhalo[step, 1, 1])
+
+    def sides(step, src):
+        left, right = v_copies(step, src)[2:]
         left.wait_recv()
         right.wait_recv()
         edge = [
@@ -209,64 +204,121 @@
         ]
         to_points(6, edge[0], edge[1])
 
+    def halo_rows(step, src):
+        up, down = v_copies(step, src)[:2]
+
+        @pl.when(has_below)
+        def _():
+            up.wait_recv()
+
+        to_points(0, vhalo[step, 0, 0], vhalo[step, 0, 1])
+
+        @pl.when(has_above)
+        def _():
+            down.wait_recv()
+
+        to_points(4, vhalo[step, 1, 0], vhalo[step, 1, 1])
+
     is_first, is_last = lane == 0, lane == 127
 
-    def stencil(i, carry):
-        rows = pl.ds(pl.multiple_of(i * SUB, SUB), SUB)
-        per = pts // SUB
-        j = lax.div(i, per)
-        sub = pl.ds(pl.multiple_of(lax.rem(i, per) * SUB, SUB), SUB)
-        uy = [u[k, rows, :] for k in range(8)]
-        ky = [kfull[j, k, sub, :] for k in range(4)]
-        fy = [ky[k] * (uy[k + 2] - uy[k]) for k in range(4)]
-        for r in range(2):
-            mid, end = uy[2 + r], uy[6 + r]
+    tile = min(pts, TILE)
+
+    def across(j, i):
+        rows = pl.ds(pl.multiple_of(j * pts + i * tile, tile), tile)
+        sub = pl.ds(i * tile, tile)
+        for r in range(2):
+            mid, end = u[2 + r, rows, :], u[6 + r, rows, :]
             a, b = pltpu.roll(mid, 127, 1), pltpu.roll(end, 127, 1)
             e, f = pltpu.roll(mid, 1, 1), pltpu.roll(end, 1, 1)
-            fx = ky[1 + r] * (jnp.where(is_last, b, a) - jnp.where(is_first, f, e))
+            fx = kfull[j, 1 + r, sub, :] * (jnp.where(is_last, b, a) - jnp.where(is_first, f, e))
             fe = kedge[j, r, sub, :] * (jnp.where(is_last, a, b) - jnp.where(is_first, e, f))
             nxt = jnp.where(is_last, pltpu.roll(fe, 127, 1), pltpu.roll(fx, 127, 1))
             prv = jnp.where(is_first, pltpu.roll(fe, 1, 1), pltpu.roll(fx, 1, 1))
-            high, low = split((nxt - prv) + (fy[r + 2] - fy[r]))
+            d_x[r, rows, :] = nxt - prv
+
+    def along(j, i):
+        rows = pl.ds(pl.multiple_of(j * pts + i * tile, tile), tile)
+        sub = pl.ds(i * tile, tile)
+        uy = [u[k, rows, :] for k in range(6)]
+        fy = [kfull[j, k, sub, :] * (uy[k + 2] - uy[k]) for k in range(4)]
+        for r in range(2):
+            high, low = split(d_x[r, rows, :] + (fy[r + 2] - fy[r]))
             d_h[rows, r * 128 : r * 128 + 128] = high
             d_l[rows, r * 128 : r * 128 + 128] = low
-        return carry
-
-    def update(src, dst):
-        lax.fori_loop(0, points // SUB, stencil, 0)
+
+    def chunk(part, j):
+        for i in range(pts // tile):
+            part(j, i)
+
+    def update(src, store):
         div = dot3(bt_h[...], bt_l[...], d_h[...], d_l[...])
         for r in range(2):
-            v = src[r]
-            dst[r] = v + relax_rate * (adj_ref[r] - (mass_shift * v - div[:, r * 128 : r * 128 + 128]))
-
-    for d in range(1, n):
-        j = lax.rem(z + d, n)
+            v = src[r, :modes]
+            store(r, v + relax_rate * (adj_ref[:, r, :] - (mass_shift * v - div[:modes, r * 128 : r * 128 + 128])))
+
+    def receive(d):
+        j = lax.rem(z + n - d, n)
         remote(coef_ref.at[j], kfull.at[j, pl.ds(1, 2)], main_send.at[j], main_recv.at[j], {"chaos": j}).wait_recv()
         forward(j)
-    fields(0, lam_ref)
-
-    def arrive(j, carry):
+
+    receive(1)
+    third = n // 2
+
+    own(lam_ref)
+    for d in range(2, third + 1):
+        receive(d)
+    sides(0, lam_ref)
+    halo_rows(0, lam_ref)
+    for d in range(max(2, third + 1), n):
+        receive(d)
+
+    def arrive(d, carry):
+        j = lax.rem(z + n - d, n)
         up, down, left, right = fwd_copies(j)
-
-        @pl.when(has_below)
-        def _():
-            up.wait_recv()
-
-        @pl.when(has_above)
-        def _():
-            down.wait_recv()
-
         left.wait_recv()
         right.wait_recv()
         for r in range(2):
             kedge[j, r] = jnp.concatenate([krecv[j, 1, r], jnp.zeros((112, pts), f32), krecv[j, 0, r]], 0).T
+        chunk(across, j)
+
+        @pl.when(has_below)
+        def _():
+            up.wait_recv()
+
+        @pl.when(has_above)
+        def _():
+            down.wait_recv()
+
+        chunk(along, j)
         return carry
 
     lax.fori_loop(0, n, arrive, 0)
-    update(lam_ref, lam1)
+
+    def keep_lam(r, value):
+        lam1[r, :modes] = value
+        lam1[r, modes:] = jnp.zeros((rows_p - modes, 128), f32)
+
+    def give(r, value):
+        out_ref[:, r, :] = value
+
+    fetch.wait()
+    update(lam_ref, keep_lam)
     start_v(1, lam1)
-    fields(1, lam1)
-    update(lam1, out_ref)
+    own(lam1)
+    sides(1, lam1)
+
+    def wide_again(j, carry):
+        chunk(across, j)
+        return carry
+
+    def tall_again(j, carry):
+        chunk(along, j)
+        return carry
+
+    lax.fori_loop(0, n, wide_again, 0)
+    halo_rows(1, lam1)
+    lax.fori_loop(0, n, tall_again, 0)
+    update(lam1, give)
 
     for d in range(1, n):
         main_copy(lax.rem(z + d, n)).wait_send()
@@ -303,20 +355,18 @@
     wide = -(-modes // 128) * 128
     dims = (n, ncore, ngx, inputs, modes, rows_p, wide, points, pts)
 
-    def by_row(v):
-        return jnp.pad(jnp.transpose(v, (1, 0, 2)), ((0, 0), (0, rows_p - modes), (0, 0)))
-
-    coef = jnp.transpose(coef_points, (1, 2, 0, 3))
-    quad = jnp.pad(quad_index, ((0, 0), (0, 128 - inputs)))
-    mode = jnp.pad(mode_index.T, ((0, 16 - inputs), (0, wide - modes)))
     vmem = pl.BlockSpec(memory_space=pltpu.VMEM)
     dma = pltpu.SemaphoreType.DMA
     out = pl.pallas_call(
         functools.partial(kernel, dims),
-        out_shape=jax.ShapeDtypeStruct((2, rows_p, 128), f32),
-        in_specs=[vmem] * 5,
+        out_shape=jax.ShapeDtypeStruct((modes, 2, 128), f32),
+        in_specs=[vmem, pl.BlockSpec(memory_space=pltpu.HBM), vmem, vmem, vmem],
         out_specs=vmem,
         scratch_shapes=[
+            pltpu.VMEM(lam_start.shape, f32),
+            pltpu.SemaphoreType.DMA,
+            pltpu.VMEM((2, rows_p, 128), f32),
+            pltpu.VMEM((16, wide), f32),
             pltpu.VMEM((n, 4, pts, 128), f32),
             pltpu.VMEM((n, 2, pts, 128), f32),
             pltpu.VMEM((n, 2, 2, 8, pts), f32),
@@ -333,13 +383,14 @@
             pltpu.VMEM((rows_p, points), bf16),
             pltpu.VMEM((points, 256), bf16),
             pltpu.VMEM((points, 256), bf16),
+            pltpu.VMEM((2, points, 128), f32),
             dma((n,)), dma((n,)), dma((4, n)), dma((4, n)), dma((STEPS, 4)), dma((STEPS, 4)),
         ],
         compiler_params=pltpu.CompilerParams(
             collective_id=0, has_side_effects=True, vmem_limit_bytes=40 * 1024 * 1024
         ),
-    )(by_row(lam_start), by_row(adj_source), coef, quad, mode)
-    return jnp.transpose(out[:, :modes], (1, 0, 2))
+    )(lam_start, adj_source, jnp.transpose(coef_points, (1, 2, 0, 3)), quad_index, mode_index.T)
+    return out
 
 
 def solution(mesh):

time: 42.7 us -> 38.2 us (0.89)
  Pallas kernels: 37.4 us -> 35.2 us
  local copies, waits for them, and re-layouts: 4.92 us -> 2.83 us
    pallas_call x1, Pallas kernels: 37.4 us -> 35.2 us  [local(): pl.pallas_call(functools.partial(kernel, dims), out_shape=jax.ShapeDtypeS...]
    transpose x2 -> x0, local copies, waits for them, and re-layouts: 0.96 us -> none  [local(): return jnp.transpose(out[:, :modes], (1, 0, 2))]
    pad x4 -> x0, local copies, waits for them, and re-layouts: 0.82 us -> none  [the longest x1 0.75 us: local(): mode = jnp.pad(mode_index.T, ((0, 16 - inputs), (0, wide - modes)))]
    unnamed x12 -> x9, local copies, waits for them, and re-layouts: 3.15 us -> 2.83 us
where the time goes in v3:
time: 38.2 us; the launch traced here: 38.1 us
  Pallas kernels  35.2 us (92%)
  local copies, waits for them, and re-layouts  2.83 us (7%)
    pallas_call x1, Pallas kernels, local(): pl.pallas_call(functools.partial(kernel, dims), out_shape=jax.ShapeDtypeS...  35.2 us
    unnamed x9, local copies, waits for them, and re-layouts  2.83 us

profile of v3, /device:TPU:9, one launch (start us, length us, event | category | flops | bytes accessed | tf_op | source)
XLA Modules:
  0.0 38.1 jit_solution(501514735298315567)
XLA Ops:
  0.0 0.9 %copy.7.quad_ref = s32[512,10]{1,0:T(8,128)S(1)} copy(s32[512,10]{0,1:T(8,128)} %param.8) | data formatting | bytes 40960 | tf_op args[3]
  0.9 0.0 copy-start
  0.9 0.0 copy-start.1
  0.9 0.0 copy-start.2
  0.9 1.2 %copy.9 = f32[128,4,2,128]{3,0,2,1:T(8,128)S(1)} copy(f32[128,4,2,128]{3,2,1,0:T(2,128)} %param.7) | data formatting | bytes 1048576 | tf_op args[2]
  2.1 0.0 copy-done
  2.1 0.0 copy-done.1
  2.2 0.0 copy-done.2
  2.2 35.2 %shard_map.55 = f32[286,2,128]{2,1,0:T(2,128)S(1)} custom-call(f32[286,2,128]{2,1,0:T(2,128)S(1)} %copy-done, f32[286,2,128]{2,1,0:T(2,128)S(1)} %copy-done.1, f32[4,2,128,128]{3,2,1,0:T(8,128)S(1)} %bitcast.4, s32[512,10]{1,0:T(8,128)S(1)} %copy.7.quad_ref, s32[10,286]{1,0:T(8,128)S(1)} %bitcast.5), custom_call_target="tpu_custom_call" | custom-call | tf_op jit(solution)/shard_map/pallas_call | solution.py:360
  37.3 0.7 %copy.11 = f32[286,2,128]{2,1,0:T(2,128)} copy(f32[286,2,128]{2,1,0:T(2,128)S(1)} %shard_map.55) | data formatting | bytes 585728
Async XLA Ops:
  0.9 1.2 %copy-start = (f32[286,2,128]{2,1,0:T(2,128)S(1)}, f32[286,2,128]{2,1,0:T(2,128)}, u32[]{:S(2)}) copy-start(f32[286,2,128]{2,1,0:T(2,128)} %lam_raw.1) | copy-start | bytes 878596
  0.9 1.2 %copy-start.1 = (f32[286,2,128]{2,1,0:T(2,128)S(1)}, f32[286,2,128]{2,1,0:T(2,128)}, u32[]{:S(2)}) copy-start(f32[286,2,128]{2,1,0:T(2,128)} %adj_hbm.1) | copy-start | bytes 878596
  0.9 1.2 %copy-start.2 = (s32[286,10]{0,1:T(8,128)S(1)}, s32[286,10]{0,1:T(8,128)}, u32[]{:S(2)}) copy-start(s32[286,10]{0,1:T(8,128)} %param.9) | copy-start | bytes 34324

commit v4 on v3

--- a/solution.py
+++ b/solution.py
@@ -315,9 +315,9 @@
         chunk(along, j)
         return carry
 
-    lax.fori_loop(0, n, wide_again, 0)
+    lax.fori_loop(0, n, wide_again, 0, unroll=n <= 4)
     halo_rows(1, lam1)
-    lax.fori_loop(0, n, tall_again, 0)
+    lax.fori_loop(0, n, tall_again, 0, unroll=n <= 4)
     update(lam1, give)
 
     for d in range(1, n):

time: 38.2 us -> 37.1 us (0.971)
  Pallas kernels: 35.2 us -> 34 us
    pallas_call x1, Pallas kernels: 35.2 us -> 34 us  [local(): pl.pallas_call(functools.partial(kernel, dims), out_shape=jax.ShapeDtypeS...]
where the time goes in v4:
time: 37.1 us; the launch traced here: 36.9 us
  Pallas kernels  34 us (92%)
  local copies, waits for them, and re-layouts  2.83 us (8%)
    pallas_call x1, Pallas kernels, local(): pl.pallas_call(functools.partial(kernel, dims), out_shape=jax.ShapeDtypeS...  34 us
    unnamed x9, local copies, waits for them, and re-layouts  2.83 us

profile of v4, /device:TPU:9, one launch (start us, length us, event | category | flops | bytes accessed | tf_op | source)
XLA Modules:
  0.0 36.9 jit_solution(6724927264645109069)
XLA Ops:
  0.0 0.9 %copy.7.quad_ref = s32[512,10]{1,0:T(8,128)S(1)} copy(s32[512,10]{0,1:T(8,128)} %param.8) | data formatting | bytes 40960 | tf_op args[3]
  0.9 0.0 copy-start
  0.9 0.0 copy-start.1
  0.9 0.0 copy-start.2
  0.9 1.2 %copy.9 = f32[128,4,2,128]{3,0,2,1:T(8,128)S(1)} copy(f32[128,4,2,128]{3,2,1,0:T(2,128)} %param.7) | data formatting | bytes 1048576 | tf_op args[2]
  2.1 0.0 copy-done
  2.1 0.0 copy-done.1
  2.2 0.0 copy-done.2
  2.2 34.0 %shard_map.55 = f32[286,2,128]{2,1,0:T(2,128)S(1)} custom-call(f32[286,2,128]{2,1,0:T(2,128)S(1)} %copy-done, f32[286,2,128]{2,1,0:T(2,128)S(1)} %copy-done.1, f32[4,2,128,128]{3,2,1,0:T(8,128)S(1)} %bitcast.4, s32[512,10]{1,0:T(8,128)S(1)} %copy.7.quad_ref, s32[10,286]{1,0:T(8,128)S(1)} %bitcast.5), custom_call_target="tpu_custom_call" | custom-call | tf_op jit(solution)/shard_map/pallas_call | solution.py:360
  36.1 0.7 %copy.11 = f32[286,2,128]{2,1,0:T(2,128)} copy(f32[286,2,128]{2,1,0:T(2,128)S(1)} %shard_map.55) | data formatting | bytes 585728
Async XLA Ops:
  0.9 1.2 %copy-start = (f32[286,2,128]{2,1,0:T(2,128)S(1)}, f32[286,2,128]{2,1,0:T(2,128)}, u32[]{:S(2)}) copy-start(f32[286,2,128]{2,1,0:T(2,128)} %lam_raw.1) | copy-start | bytes 878596
  0.9 1.2 %copy-start.1 = (f32[286,2,128]{2,1,0:T(2,128)S(1)}, f32[286,2,128]{2,1,0:T(2,128)}, u32[]{:S(2)}) copy-start(f32[286,2,128]{2,1,0:T(2,128)} %adj_hbm.1) | copy-start | bytes 878596
  0.9 1.2 %copy-start.2 = (s32[286,10]{0,1:T(8,128)S(1)}, s32[286,10]{0,1:T(8,128)}, u32[]{:S(2)}) copy-start(s32[286,10]{0,1:T(8,128)} %param.9) | copy-start | bytes 34324
